TPU v7x, 512 devices: a whole 4x8x8 slice. The times are simulated.
512 devices in a mesh: row: 32 (over y, x), col: 16 (over z, core).
Axes of the slice: x: 4, y: 8, z: 8, core: 2. Of those that a mesh axis runs over, the one named last changes fastest.
Arguments:
- activations: bfloat16 [384, 8192], P('row', 'col'), may hold values from -6 to 6
- gate_weight: bfloat16 [8192, 16384], P('col', 'row'), may hold values from -0.0625 to 0.0625
- up_weight: bfloat16 [8192, 16384], P('col', 'row'), may hold values from -0.0625 to 0.0625
- down_weight: bfloat16 [16384, 8192], P('row', 'col'), may hold values from -0.046875 to 0.046875
- out_grad: bfloat16 [384, 8192], P('row', 'col'), may hold values from -1.75 to 1.75
Outputs:
- layer_out: bfloat16 [384, 8192], P('row', 'col')
- input_grad: bfloat16 [384, 8192], P('row', 'col')
- gate_grad: float32 [8192, 16384], P('col', 'row')
- up_grad: float32 [8192, 16384], P('col', 'row')
- down_grad: float32 [16384, 8192], P('row', 'col')
All inputs are finite; a program needn't handle non-finite values.
Results may differ from a plain program's by a relative error of at most 0.005.
Values may be sent and summed in bfloat16 or wider, within the bound.
No kernel may reach another device: no remote copies, remote signals or barrier semaphores. Data moves between devices by JAX's collectives and lax.ppermute only.
A program may use at most 64 MiB of HBM per device.

v0:
```python
import jax
import jax.numpy as jnp
from jax import lax
from jax.sharding import PartitionSpec as P


def contract_rows(left_side, right_side):
    return lax.dot_general(
        left_side, right_side, (((0,), (0,)), ((), ())), preferred_element_type=jnp.float32
    )


def contract_cols(left_side, right_side):
    return lax.dot_general(
        left_side, right_side, (((1,), (1,)), ((), ())), preferred_element_type=jnp.float32
    )


def swiglu_deltas(hidden_grad, gate, up):
    gate_sigmoid = jax.nn.sigmoid(gate)
    gate_silu = gate * gate_sigmoid
    gate_delta = (hidden_grad * up * gate_sigmoid * (1.0 + gate * (1.0 - gate_sigmoid))).astype(
        jnp.bfloat16
    )
    up_delta = (hidden_grad * gate_silu).astype(jnp.bfloat16)
    return (gate_delta, up_delta)


def local(activations, gate_weight, up_weight, down_weight, out_grad):
    hidden_width = gate_weight.shape[1]
    feature_width = activations.shape[1]
    all_tokens, all_grads = (
        lax.all_gather(activations, "row", axis=0, tiled=True),
        lax.all_gather(out_grad, "row", axis=0, tiled=True),
    )
    both_weights = jnp.concatenate([gate_weight, up_weight], axis=1)
    picked = all_tokens
    summed = lax.psum_scatter(
        jnp.dot(picked, both_weights, preferred_element_type=jnp.float32),
        "col",
        scatter_dimension=0,
        tiled=True,
    )
    gate = summed[:, :hidden_width]
    up = summed[:, hidden_width:]
    hidden = (jax.nn.silu(gate) * up).astype(jnp.bfloat16)
    hidden_all = lax.all_gather(hidden, "col", axis=0, tiled=True)
    picked = all_grads
    hidden_grad = lax.psum_scatter(
        contract_cols(picked, down_weight), "col", scatter_dimension=0, tiled=True
    )
    gate_delta, up_delta = swiglu_deltas(hidden_grad, gate, up)
    all_gate_delta, all_up_delta = (
        lax.all_gather(gate_delta, "col", axis=0, tiled=True),
        lax.all_gather(up_delta, "col", axis=0, tiled=True),
    )
    gate_grad = contract_rows(all_tokens, all_gate_delta)
    up_grad = contract_rows(all_tokens, all_up_delta)
    down_grad = contract_rows(hidden_all, all_grads)
    forward_term = jnp.dot(hidden_all, down_weight, preferred_element_type=jnp.float32)
    backward_term = contract_cols(all_gate_delta, gate_weight) + contract_cols(
        all_up_delta, up_weight
    )
    row_total = lax.psum_scatter(
        jnp.concatenate([forward_term, backward_term], axis=1),
        "row",
        scatter_dimension=0,
        tiled=True,
    )
    layer_out = row_total[:, :feature_width].astype(jnp.bfloat16)
    input_grad = row_total[:, feature_width:].astype(jnp.bfloat16)
    return (layer_out, input_grad, gate_grad, up_grad, down_grad)


def solution(mesh):
    return jax.shard_map(
        local,
        mesh=mesh,
        in_specs=(
            P("row", "col"),
            P("col", "row"),
            P("col", "row"),
            P("row", "col"),
            P("row", "col"),
        ),
        out_specs=(
            P("row", "col"),
            P("row", "col"),
            P("col", "row"),
            P("col", "row"),
            P("row", "col"),
        ),
        check_vma=False,
    )
```

profile of v0, /device:TPU:64, one launch (start us, length us, event | category | flops | bytes accessed | tf_op | source)
XLA Modules:
  0.0 370.0 jit_solution(8546678322941645992)
XLA Ops:
  7.2 50.6 %all-gather.1 = bf16[32,12,512]{2,1,0:T(8,128)(2,1)S(1)} all-gather(bf16[1,12,512]{2,1,0:T(8,128)(2,1)} %bitcast.28), channel_id=1, replica_groups=mesh['row'=32,'col'=16] {'row'}, dimensions={0}, use_global_device_ids=true | all-gather | bytes 405504 | tf_op jit(solution)/shard_map/all_gather | solution.py:34
  58.0 1.3 fusion.9
  59.3 48.1 %all-gather = bf16[32,12,512]{2,1,0:T(8,128)(2,1)S(1)} all-gather(bf16[1,12,512]{2,1,0:T(8,128)(2,1)S(1)} %bitcast.29), channel_id=1, replica_groups=mesh['row'=32,'col'=16] {'row'}, dimensions={0}, use_global_device_ids=true | all-gather | bytes 405504 | tf_op jit(solution)/shard_map/all_gather | solution.py:33
  107.6 1.8 convolution_bitcast_fusion
  109.4 1.6 copy.30
  111.1 1.3 dynamic-slice.4
  113.0 4.8 %reduce-scatter.11.cloned.1.call-done = f32[24,512]{1,0:T(8,128)} async-done(((f32[384,512]{1,0:T(8,128)}), f32[24,512]{1,0:T(8,128)}) %reduce-scatter.11.cloned.1.call-update) | async-done | bytes 49168 | tf_op jit(solution)/shard_map/reduce_scatter | solution.py:49
  117.9 62.4 %reduce-scatter.9.cloned.1.call-done = f32[24,1024]{1,0:T(8,128)} async-done(((f32[384,1024]{1,0:T(8,128)}), f32[24,1024]{1,0:T(8,128)}) %reduce-scatter.9.cloned.1.call-update) | async-done | bytes 98320 | tf_op jit(solution)/shard_map/reduce_scatter | solution.py:38
  181.1 18.8 %all_gather.18 = bf16[384,512]{1,0:T(8,128)(2,1)S(1)} all-gather(bf16[24,512]{1,0:T(8,128)(2,1)S(1)} %get-tuple-element.26), channel_id=1, replica_groups=mesh['row'=32,'col'=16] {'col'}, dimensions={0}, use_global_device_ids=true | all-gather | bytes 417792 | tf_op jit(solution)/shard_map/all_gather | solution.py:54
  200.3 15.4 %all_gather.19 = bf16[384,512]{1,0:T(8,128)(2,1)S(1)} all-gather(bf16[24,512]{1,0:T(8,128)(2,1)S(1)} %get-tuple-element.25), channel_id=1, replica_groups=mesh['row'=32,'col'=16] {'col'}, dimensions={0}, use_global_device_ids=true | all-gather | bytes 417792 | tf_op jit(solution)/shard_map/all_gather | solution.py:55
  215.8 17.1 %all_gather.16 = bf16[384,512]{1,0:T(8,128)(2,1)S(1)} all-gather(bf16[24,512]{1,0:T(8,128)(2,1)S(1)} %get-tuple-element.27), channel_id=1, replica_groups=mesh['row'=32,'col'=16] {'col'}, dimensions={0}, use_global_device_ids=true | all-gather | bytes 417792 | tf_op jit(solution)/shard_map/all_gather | solution.py:47
  234.2 88.3 %fusion = f32[16,1024]{1,0:T(8,128)S(1)} fusion(f32[384,1024]{1,0:T(8,128)S(1)} %pad_maximum_fusion), kind=kCustom, calls=%all-reduce-scatter | all-reduce-scatter fusion | flops 524289 | bytes 1640448
  322.4 1.3 collective-permute-start
  323.7 1.3 collective-permute-start.1
  325.0 1.9 collective-permute-start.2
  326.9 1.9 collective-permute-start.3
  329.3 10.8 %collective-permute-start.7 = (bf16[12,1024]{1,0:T(8,128)(2,1)S(1)}, bf16[12,1024]{1,0:T(8,128)(2,1)S(1)}, u32[]{:S(2)}, u32[]{:S(2)}) collective-permute-start(bf16[12,1024]{1,0:T(8,128)(2,1)S(1)} %slice.22), channel_id=1, source_target_pairs={{0,128},{16,144},{32,160},{48,176},{64,192},{80,208},{96,224},{112... | collective-permute-start | bytes 73736
  341.7 2.2 collective-permute-start.4
  343.9 6.0 %collective-permute-start.5 = (bf16[16,1024]{1,0:T(8,128)(2,1)S(1)}, bf16[16,1024]{1,0:T(8,128)(2,1)S(1)}, u32[]{:S(2)}, u32[]{:S(2)}) collective-permute-start(bf16[16,1024]{1,0:T(8,128)(2,1)S(1)} %convert.20), channel_id=1, source_target_pairs={{0,96},{16,112},{32,128},{48,144},{64,160},{80,176},{96,192},{112,... | collective-permute-start | bytes 98312
  350.0 5.8 %collective-permute-start.6 = (bf16[16,1024]{1,0:T(8,128)(2,1)S(1)}, bf16[16,1024]{1,0:T(8,128)(2,1)S(1)}, u32[]{:S(2)}, u32[]{:S(2)}) collective-permute-start(bf16[16,1024]{1,0:T(8,128)(2,1)S(1)} %convert.20), channel_id=1, source_target_pairs={{0,112},{16,128},{32,144},{48,160},{64,176},{80,192},{96,208},{112... | collective-permute-start | bytes 98312
  355.8 1.4 fusion.11
  357.2 1.3 copy.27
  358.6 1.3 copy.28
  359.9 2.6 concatenate.8
  (51 shorter events, 5.6 us)
Async XLA Ops:
  7.2 50.8 %copy-start = (bf16[512,512]{1,0:T(8,128)(2,1)S(1)}, bf16[512,512]{1,0:T(8,128)(2,1)}, u32[]{:S(2)}) copy-start(bf16[512,512]{1,0:T(8,128)(2,1)} %param.8) | copy-start | bytes 1572868
  7.2 110.7 %reduce-scatter.11.cloned.1.call-start = ((), (), s32[]{:S(2)}) async-start(), calls=%async_computation.3 | async-start | bytes 835584 | tf_op jit(solution)/shard_map/reduce_scatter | solution.py:49
  57.8 1.5 copy-start.12
  57.9 49.6 %copy-start.1 = (bf16[384,512]{1,0:T(8,128)(2,1)}, bf16[384,512]{1,0:T(8,128)(2,1)S(1)}, u32[]{:S(2)}) copy-start(bf16[384,512]{1,0:T(8,128)(2,1)S(1)} %reshape.13) | copy-start | bytes 1179652
  57.9 49.6 %copy-start.5 = (bf16[512,512]{1,0:T(8,128)(2,1)S(1)}, bf16[512,512]{1,0:T(8,128)(2,1)}, u32[]{:S(2)}) copy-start(bf16[512,512]{1,0:T(8,128)(2,1)} %param.7) | copy-start | bytes 1572868
  59.3 121.0 %reduce-scatter.9.cloned.1.call-start = ((), (), s32[]{:S(2)}) async-start(), calls=%async_computation.2 | async-start | bytes 1671168 | tf_op jit(solution)/shard_map/reduce_scatter | solution.py:38
  111.0 88.9 %copy-start.7 = (bf16[512,512]{1,0:T(8,128)(2,1)S(1)}, bf16[512,512]{1,0:T(8,128)(2,1)}, u32[]{:S(2)}) copy-start(bf16[512,512]{1,0:T(8,128)(2,1)} %param.6) | copy-start | bytes 1572868
  200.3 33.3 %copy-start.6 = (bf16[512,512]{1,0:T(8,128)(2,1)S(1)}, bf16[512,512]{1,0:T(8,128)(2,1)}, u32[]{:S(2)}) copy-start(bf16[512,512]{1,0:T(8,128)(2,1)} %param.7) | copy-start | bytes 1572868
  232.9 0.7 copy-start.3
  322.4 21.5 %collective-permute-start = (bf16[16,1024]{1,0:T(8,128)(2,1)S(1)}, bf16[16,1024]{1,0:T(8,128)(2,1)S(1)}, u32[]{:S(2)}, u32[]{:S(2)}) collective-permute-start(bf16[16,1024]{1,0:T(8,128)(2,1)S(1)} %convert.20), channel_id=1, source_target_pairs={{0,16},{16,32},{32,48},{48,64},{64,80},{80,96},{96,112},{112,128},... | collective-permute-start | bytes 98312
  323.7 26.2 %collective-permute-start.1 = (bf16[16,1024]{1,0:T(8,128)(2,1)S(1)}, bf16[16,1024]{1,0:T(8,128)(2,1)S(1)}, u32[]{:S(2)}, u32[]{:S(2)}) collective-permute-start(bf16[16,1024]{1,0:T(8,128)(2,1)S(1)} %convert.20), channel_id=1, source_target_pairs={{0,32},{16,48},{32,64},{48,80},{64,96},{80,112},{96,128},{112,144}... | collective-permute-start | bytes 98312
  325.0 34.8 %collective-permute-start.2 = (bf16[16,1024]{1,0:T(8,128)(2,1)S(1)}, bf16[16,1024]{1,0:T(8,128)(2,1)}, u32[]{:S(2)}, u32[]{:S(2)}) collective-permute-start(bf16[16,1024]{1,0:T(8,128)(2,1)S(1)} %convert.20), channel_id=1, source_target_pairs={{0,48},{16,64},{32,80},{48,96},{64,112},{80,128},{96,144},{112,160... | collective-permute-start | bytes 98312
  326.9 32.9 %collective-permute-start.3 = (bf16[16,1024]{1,0:T(8,128)(2,1)S(1)}, bf16[16,1024]{1,0:T(8,128)(2,1)}, u32[]{:S(2)}, u32[]{:S(2)}) collective-permute-start(bf16[16,1024]{1,0:T(8,128)(2,1)S(1)} %convert.20), channel_id=1, source_target_pairs={{0,64},{16,80},{32,96},{48,112},{64,128},{80,144},{96,160},{112,17... | collective-permute-start | bytes 98312
  328.8 27.0 %copy-start.2 = (bf16[384,512]{1,0:T(8,128)(2,1)S(1)}, bf16[384,512]{1,0:T(8,128)(2,1)}, u32[]{:S(2)}) copy-start(bf16[384,512]{1,0:T(8,128)(2,1)} %copy-done.1) | copy-start | bytes 1179652
  328.9 27.0 %copy-start.4 = (bf16[384,512]{1,0:T(8,128)(2,1)S(1)}, bf16[384,512]{1,0:T(8,128)(2,1)}, u32[]{:S(2)}) copy-start(bf16[384,512]{1,0:T(8,128)(2,1)} %copy-done.3) | copy-start | bytes 1179652
  329.3 12.4 %collective-permute-start.7 = (bf16[12,1024]{1,0:T(8,128)(2,1)S(1)}, bf16[12,1024]{1,0:T(8,128)(2,1)S(1)}, u32[]{:S(2)}, u32[]{:S(2)}) collective-permute-start(bf16[12,1024]{1,0:T(8,128)(2,1)S(1)} %slice.22), channel_id=1, source_target_pairs={{0,128},{16,144},{32,160},{48,176},{64,192},{80,208},{96,224},{112... | collective-permute-start | bytes 73736
  341.7 14.1 %copy-start.10 = (bf16[12,1024]{1,0:T(8,128)(2,1)}, bf16[12,1024]{1,0:T(8,128)(2,1)S(1)}, u32[]{:S(2)}) copy-start(bf16[12,1024]{1,0:T(8,128)(2,1)S(1)} %collective-permute-done.7) | copy-start | bytes 73732
  341.7 18.2 %collective-permute-start.4 = (bf16[16,1024]{1,0:T(8,128)(2,1)S(1)}, bf16[16,1024]{1,0:T(8,128)(2,1)S(1)}, u32[]{:S(2)}, u32[]{:S(2)}) collective-permute-start(bf16[16,1024]{1,0:T(8,128)(2,1)S(1)} %convert.20), channel_id=1, source_target_pairs={{0,80},{16,96},{32,112},{48,128},{64,144},{80,160},{96,176},{112,1... | collective-permute-start | bytes 98312
  343.9 15.9 %collective-permute-start.5 = (bf16[16,1024]{1,0:T(8,128)(2,1)S(1)}, bf16[16,1024]{1,0:T(8,128)(2,1)S(1)}, u32[]{:S(2)}, u32[]{:S(2)}) collective-permute-start(bf16[16,1024]{1,0:T(8,128)(2,1)S(1)} %convert.20), channel_id=1, source_target_pairs={{0,96},{16,112},{32,128},{48,144},{64,160},{80,176},{96,192},{112,... | collective-permute-start | bytes 98312
  350.0 5.8 %copy-start.8 = (bf16[16,1024]{1,0:T(8,128)(2,1)}, bf16[16,1024]{1,0:T(8,128)(2,1)S(1)}, u32[]{:S(2)}) copy-start(bf16[16,1024]{1,0:T(8,128)(2,1)S(1)} %collective-permute-done.1) | copy-start | bytes 98308
  350.0 9.9 %collective-permute-start.6 = (bf16[16,1024]{1,0:T(8,128)(2,1)S(1)}, bf16[16,1024]{1,0:T(8,128)(2,1)S(1)}, u32[]{:S(2)}, u32[]{:S(2)}) collective-permute-start(bf16[16,1024]{1,0:T(8,128)(2,1)S(1)} %convert.20), channel_id=1, source_target_pairs={{0,112},{16,128},{32,144},{48,160},{64,176},{80,192},{96,208},{112... | collective-permute-start | bytes 98312
  358.6 1.3 copy-start.9
  358.6 1.4 copy-start.11
Sparse Core Ops, SparseCore 0:
  59.4 58.4 reduce-scatter.10
  120.9 59.2 reduce-scatter.8
where the time goes:
time: 371 us; the launch traced here: 370 us
  blocking collectives  238 us (64%)
  waiting for transfers between devices  68.4 us (18%)
  starting transfers between devices  31.3 us (8%)
  between operations  15 us (4%)
  local copies, waits for them, and re-layouts  9.43 us (3%)
  matrix products  6.56 us (2%)
    unnamed x1, blocking collectives  88.3 us
    reduce_scatter x1, waiting for transfers between devices, local(): lax.psum_scatter(jnp.dot(picked, both_weights, preferred_element_type=jnp...  62.4 us
    all_gather x1, blocking collectives, local(): lax.all_gather(out_grad, 'row', axis=0, tiled=True)  50.6 us
    all_gather x1, blocking collectives, local(): lax.all_gather(activations, 'row', axis=0, tiled=True)  48.1 us
    unnamed x8, starting transfers between devices  31.2 us
    all_gather x1, blocking collectives, local(): lax.all_gather(gate_delta, 'col', axis=0, tiled=True)  18.8 us
    all_gather x1, blocking collectives, local(): hidden_all = lax.all_gather(hidden, 'col', axis=0, tiled=True)  17.1 us
    all_gather x1, blocking collectives, local(): lax.all_gather(up_delta, 'col', axis=0, tiled=True)  15.4 us
  transfers between devices with their start and end apart: 10, of which 3 were waited for; matrix products, arithmetic and copies ran while one was open for 3% of the time, Pallas kernels for 0%

commit v1 on v0

v1 whole, which is shorter than its diff:
```python
import functools

import jax
import jax.numpy as jnp
from jax import lax
from jax.experimental import pallas as pl
from jax.experimental.pallas import tpu as pltpu
from jax.sharding import Mesh, PartitionSpec as P

F32 = jnp.float32
BF16 = jnp.bfloat16
VM = pl.BlockSpec(memory_space=pltpu.VMEM)
SM = pl.BlockSpec(memory_space=pltpu.SMEM)
PARAMS = pltpu.CompilerParams(vmem_limit_bytes=40 * 2**20)


def mm(left, right):
    return jnp.dot(left, right, preferred_element_type=F32)


def mm_t(left, right):
    return lax.dot_general(left, right, (((1,), (1,)), ((), ())), preferred_element_type=F32)


def t_mm(left, right):
    return lax.dot_general(left, right, (((0,), (0,)), ((), ())), preferred_element_type=F32)


def spread(block, axis, size):
    return lax.all_to_all(jnp.broadcast_to(block[None], (size,) + block.shape), axis, 0, 0)


def add_up(blocks):
    total = blocks[0].astype(F32)
    for i in range(1, blocks.shape[0]):
        total = total + blocks[i].astype(F32)
    return total


def low_rows(shape):
    return lax.broadcasted_iota(jnp.int32, shape, 1) < 4


def pack_kernel(a, b, out):
    head = (a[:8], b[:8])
    tail = jnp.concatenate([a[8:].astype(F32), b[8:].astype(F32)], axis=0).astype(BF16)
    for i in range(out.shape[0]):
        out[i, 0:8, :] = head[0]
        out[i, 8:16, :] = head[1]
        out[i, 16:24, :] = tail


def pack(a, b, copies):
    return pl.pallas_call(
        pack_kernel,
        out_shape=jax.ShapeDtypeStruct((copies, 24, a.shape[1]), BF16),
        in_specs=[VM, VM],
        out_specs=VM,
        compiler_params=PARAMS,
        name="pack",
    )(a, b)


def total_kernel(blocks, layer_out, input_grad):
    total = blocks[0].astype(F32)
    for i in range(1, blocks.shape[0]):
        total = total + blocks[i].astype(F32)
    layer_out[:8] = total[:8].astype(BF16)
    layer_out[8:] = total[16:20].astype(BF16)
    input_grad[:8] = total[8:16].astype(BF16)
    input_grad[8:] = total[20:24].astype(BF16)


def totals(blocks):
    shape = jax.ShapeDtypeStruct((12, blocks.shape[2]), BF16)
    return pl.pallas_call(total_kernel, out_shape=(shape, shape), in_specs=[VM], compiler_params=PARAMS, name="totals")(blocks)


def partial_kernel(which, blocks, gate_weight, up_weight, down_weight, out, x_out, g_out):
    m = x_out.shape[0] // 12
    d = x_out.shape[1]
    rows = pl.ds(which[0] * m, m)
    tail = blocks[rows, 16:24, :].astype(F32).reshape(m // 2, 16, d)
    even, odd = tail[:, :8], tail[:, 8:]
    low = low_rows(even.shape)
    x_tail = jnp.where(low, even, pltpu.roll(odd, 4, 1)).reshape(m * 4, d)
    g_tail = jnp.where(low, pltpu.roll(even, 4, 1), odd).reshape(m * 4, d)
    x_head = blocks[rows, 0:8, :].astype(F32).reshape(m * 8, d)
    g_head = blocks[rows, 8:16, :].astype(F32).reshape(m * 8, d)
    x = jnp.concatenate([x_head, x_tail], axis=0).astype(BF16)
    g = jnp.concatenate([g_head, g_tail], axis=0).astype(BF16)
    x_out[...] = x
    g_out[...] = g
    h = gate_weight.shape[1]
    out[:, :h] = mm(x, gate_weight[...])
    out[:, h : 2 * h] = mm(x, up_weight[...])
    out[:, 2 * h :] = mm_t(g, down_weight[...])


def partial_sums(which, blocks, gate_weight, up_weight, down_weight):
    n = blocks.shape[0] * 12 // 2
    d = blocks.shape[2]
    h = gate_weight.shape[1]
    shape = jax.ShapeDtypeStruct
    return pl.pallas_call(
        partial_kernel,
        out_shape=(shape((n, 3 * h), F32), shape((n, d), BF16), shape((n, d), BF16)),
        in_specs=[SM, VM, VM, VM, VM],
        out_specs=(VM, VM, VM),
        compiler_params=PARAMS,
        cost_estimate=pl.CostEstimate(flops=2 * n * d * 3 * h, bytes_accessed=4 * n * 3 * h, transcendentals=0),
        name="partial_sums",
    )(which, blocks, gate_weight, up_weight, down_weight)


def output_kernel(which, own, other, gate_weight, up_weight, down_weight, out):
    h = gate_weight.shape[1]
    d = gate_weight.shape[0]
    for part, where in ((own, which[0]), (other, 1 - which[0])):
        m = part.shape[0] // 12
        f = mm(part[:, :h], down_weight[...])
        b = mm_t(part[:, h : 2 * h], gate_weight[...]) + mm_t(part[:, 2 * h :], up_weight[...])
        rows = pl.ds(where * m, m)
        out[rows, 0:8, :] = f[: m * 8].reshape(m, 8, d).astype(BF16)
        out[rows, 8:16, :] = b[: m * 8].reshape(m, 8, d).astype(BF16)
        f = f[m * 8 :].reshape(m // 2, 8, d)
        b = b[m * 8 :].reshape(m // 2, 8, d)
        low = low_rows(f.shape)
        even = jnp.where(low, f, pltpu.roll(b, 4, 1))
        odd = jnp.where(low, pltpu.roll(f, 4, 1), b)
        out[rows, 16:24, :] = jnp.concatenate([even, odd], axis=1).reshape(m, 8, d).astype(BF16)


def output_blocks(which, own, other, gate_weight, up_weight, down_weight):
    n, width = own.shape
    d = gate_weight.shape[0]
    return pl.pallas_call(
        output_kernel,
        out_shape=jax.ShapeDtypeStruct((n // 6, 24, d), BF16),
        in_specs=[SM, VM, VM, VM, VM, VM],
        out_specs=VM,
        compiler_params=PARAMS,
        cost_estimate=pl.CostEstimate(flops=4 * n * d * width, bytes_accessed=8 * n * d, transcendentals=0),
        name="output_blocks",
    )(which, own, other, gate_weight, up_weight, down_weight)


def local(sizes, activations, gate_weight, up_weight, down_weight, out_grad):
    ny, nx, nz, nc = sizes
    d = activations.shape[1]
    h = gate_weight.shape[1]
    rows = ny * nx
    swap = [(0, 1), (1, 0)]
    core = lax.axis_index("core").astype(jnp.int32).reshape(1)
    away = 1 - core

    both = pack(activations, out_grad, ny)
    both, core, away = lax.optimization_barrier((both, core, away))
    both = spread(lax.all_to_all(both, "y", 0, 0), "x", nx).reshape(rows, 24, d)
    weights = (gate_weight, up_weight, down_weight)
    send, x_other, g_other = partial_sums(away, both, *weights)
    sent = lax.ppermute(send, "core", swap)
    keep, x_own, g_own = partial_sums(core, both, *weights)
    half = keep.shape[0]
    n = half // nz
    chip = (keep + sent).astype(BF16).reshape(nz, n, 3 * h)
    summed = add_up(lax.all_to_all(chip, "z", 0, 0))
    gate, up, hidden_grad = summed[:, :h], summed[:, h : 2 * h], summed[:, 2 * h :]
    sig = jax.nn.sigmoid(gate)
    silu = gate * sig
    hidden = (silu * up).astype(BF16)
    gate_delta = (hidden_grad * up * sig * (1.0 + gate * (1.0 - sig))).astype(BF16)
    up_delta = (hidden_grad * silu).astype(BF16)
    mine = jnp.concatenate([hidden, gate_delta, up_delta], axis=1)
    own = spread(mine, "z", nz).reshape(half, 3 * h)
    other = lax.ppermute(own, "core", swap)
    blocks = output_blocks(core, own, other, *weights)
    layer_out, input_grad = totals(lax.all_to_all(blocks, ("x", "y"), 0, 0))

    hid, gd, ud = (jnp.concatenate([own[:, i * h : (i + 1) * h], other[:, i * h : (i + 1) * h]], axis=0) for i in range(3))
    x_cat = jnp.concatenate([x_own, x_other], axis=0)
    g_cat = jnp.concatenate([g_own, g_other], axis=0)
    return layer_out, input_grad, t_mm(x_cat, gd), t_mm(x_cat, ud), t_mm(hid, g_cat)


def solution(mesh):
    sizes = (8, 4, 8, 2)
    fine = Mesh(mesh.devices.reshape(sizes), ("y", "x", "z", "core"))
    tokens, features = ("y", "x"), ("z", "core")
    tile = P(tokens, features)
    return jax.shard_map(
        functools.partial(local, sizes),
        mesh=fine,
        in_specs=(tile, P(features, tokens), P(features, tokens), tile, tile),
        out_specs=(tile, tile, P(features, tokens), P(features, tokens), tile),
        check_vma=False,
    )
```

time: 371 us -> 125 us (0.34)
  the two profiles are of different devices: /device:TPU:64 before, /device:TPU:8 now
where the time goes in v1:
time: 125 us; the launch traced here: 124 us
  blocking collectives  80.8 us (65%)
  waiting for transfers between devices  23.1 us (18%)
  starting transfers between devices  9.59 us (8%)
  matrix products  4.3 us (3%)
  Pallas kernels  3.78 us (3%)
  local copies, waits for them, and re-layouts  1.65 us (1%)
    all_to_all x2, blocking collectives, spread(): lax.all_to_all(jnp.broadcast_to(block[None], (size,) + block.shape), axis...  35 us
    all_to_all x1, blocking collectives, local(): summed = add_up(lax.all_to_all(chip, 'z', 0, 0))  29.3 us
    all_to_all x1, waiting for transfers between devices, local(): layer_out, input_grad = totals(lax.all_to_all(blocks, ('x', 'y'), 0, 0))  18.8 us
    all_to_all x1, blocking collectives, local(): both = spread(lax.all_to_all(both, 'y', 0, 0), 'x', nx).reshape(rows, 24, d)  16.5 us
    all_to_all x1, starting transfers between devices, local(): layer_out, input_grad = totals(lax.all_to_all(blocks, ('x', 'y'), 0, 0))  5.76 us
    dot_general x3, matrix products, t_mm(): lax.dot_general(left, right, (((0,), (0,)), ((), ())), preferred_element_...  4.3 us
  transfers between devices with their start and end apart: 3, of which 3 were waited for; matrix products, arithmetic and copies ran while one was open for 4% of the time, Pallas kernels for 0%

profile of v1, /device:TPU:8, one launch (start us, length us, event | category | flops | bytes accessed | tf_op | source)
XLA Modules:
  0.0 124.2 jit_solution(1525669876518117202)
XLA Ops:
  0.6 0.0 copy-start.3
  0.6 0.7 copy-done.3
  1.4 0.7 copy-done.4
  2.1 16.5 %all_to_all.25 = bf16[8,24,512]{2,1,0:T(8,128)(2,1)S(1)} all-to-all(bf16[8,24,512]{2,1,0:T(8,128)(2,1)S(1)} %pack.1), channel_id=1, replica_groups=mesh['y'=8,'x'=4,'z'=8,'core'=2] {'y'}, dimensions={0} | all-to-all | bytes 393216 | tf_op jit(solution)/shard_map/all_to_all | solution.py:159
  18.6 0.1 broadcast_in_dim.4
  18.7 14.2 %all_to_all.26 = bf16[4,8,24,512]{3,2,1,0:T(8,128)(2,1)S(1)} all-to-all(bf16[4,8,24,512]{3,2,1,0:T(8,128)(2,1)S(1)} %broadcast_in_dim.4), channel_id=1, replica_groups=mesh['y'=8,'x'=4,'z'=8,'core'=2] {'x'}, dimensions={0} | all-to-all | bytes 1572864 | tf_op jit(solution)/shard_map/all_to_all | solution.py:30
  32.9 0.0 copy-done
  32.9 0.5 partial_sums.3
  33.5 1.9 %collective-permute-start = (f32[192,1536]{1,0:T(8,128)S(1)}, f32[192,1536]{1,0:T(8,128)S(1)}, u32[]{:S(2)}, u32[]{:S(2)}) collective-permute-start(f32[192,1536]{1,0:T(8,128)S(1)} %get-tuple-element.20), channel_id=1, source_target_pairs={{0,1},{1,0},{2,3},{3,2},{4,5},{5,4},{6,7},{7,6},{8,9},{9,8},{10,11... | collective-permute-start | bytes 3538952 | tf_op jit(solution)/shard_map/ppermute | solution.py:162
  35.4 0.5 partial_sums.2
  35.9 2.3 %collective-permute-done = f32[192,1536]{1,0:T(8,128)S(1)} collective-permute-done((f32[192,1536]{1,0:T(8,128)S(1)}, f32[192,1536]{1,0:T(8,128)S(1)}, u32[]{:S(2)}, u32[]{:S(2)}) %collective-permute-start) | collective-permute-done | bytes 1179680 | tf_op jit(solution)/shard_map/ppermute | solution.py:162
  38.2 0.1 add_convert_fusion
  38.3 29.3 %all_to_all.27 = bf16[8,24,1536]{2,1,0:T(8,128)(2,1)S(1)} all-to-all(bf16[8,24,1536]{2,1,0:T(8,128)(2,1)S(1)} %bitcast.13), channel_id=1, replica_groups=mesh['y'=8,'x'=4,'z'=8,'core'=2] {'z'}, dimensions={0} | all-to-all | bytes 1179648 | tf_op jit(solution)/shard_map/all_to_all | solution.py:167
  67.7 0.1 add_bitcast_fusion
  67.8 20.8 %all_to_all.28 = bf16[8,24,1536]{2,1,0:T(8,128)(2,1)S(1)} all-to-all(bf16[8,24,1536]{2,1,0:T(8,128)(2,1)S(1)} %broadcast_in_dim.5), channel_id=1, replica_groups=mesh['y'=8,'x'=4,'z'=8,'core'=2] {'z'}, dimensions={0} | all-to-all | bytes 1179648 | tf_op jit(solution)/shard_map/all_to_all | solution.py:30
  88.6 1.9 %collective-permute-start.1 = (bf16[192,1536]{1,0:T(8,128)(2,1)S(1)}, bf16[192,1536]{1,0:T(8,128)(2,1)S(1)}, u32[]{:S(2)}, u32[]{:S(2)}) collective-permute-start(bf16[192,1536]{1,0:T(8,128)(2,1)S(1)} %bitcast.10), channel_id=1, source_target_pairs={{0,1},{1,0},{2,3},{3,2},{4,5},{5,4},{6,7},{7,6},{8,9},{9,8},{10,11... | collective-permute-start | bytes 1769480 | tf_op jit(solution)/shard_map/ppermute | solution.py:176
  90.5 2.0 %collective-permute-done.1.other = bf16[192,1536]{1,0:T(8,128)(2,1)S(1)} collective-permute-done((bf16[192,1536]{1,0:T(8,128)(2,1)S(1)}, bf16[192,1536]{1,0:T(8,128)(2,1)S(1)}, u32[]{:S(2)}, u32[]{:S(2)}) %collective-permute-start.1) | collective-permute-done | bytes 589856 | tf_op jit(solution)/shard_map/ppermute | solution.py:176
  92.5 2.0 %output_blocks.1 = bf16[32,24,512]{2,1,0:T(8,128)(2,1)} custom-call(s32[1]{0:T(128)} %bitcast.which, bf16[192,1536]{1,0:T(8,128)(2,1)S(1)} %bitcast.11, bf16[192,1536]{1,0:T(8,128)(2,1)S(1)} %collective-permute-done.1.other, bf16[512,512]{1,0:T(8,128)(2,1)S(1)} %copy-done, bf16[512,512]{1,0:T(8,128)(2,1)S(1)} %copy-done.1, bf16[512,512]{1,0:T(8,128)(2,1)S(1)} %copy-done.2), custom_call_target="tpu_custom_call" | custom-call | flops 603979776 | bytes 786432 | tf_op jit(solution)/shard_map/output_blocks/pallas_call | solution.py:137
  94.5 5.8 %all-to-all-start.4 = ((bf16[32,24,512]{2,1,0:T(8,128)(2,1)}), bf16[32,24,512]{2,1,0:T(8,128)(2,1)S(1)}, u32[]{:S(2)}, u32[]{:S(2)}) async-start(bf16[32,24,512]{2,1,0:T(8,128)(2,1)} %output_blocks.1), calls=%async_computation.4 | async-start | bytes 1572864 | tf_op jit(solution)/shard_map/all_to_all | solution.py:178
  100.4 1.4 %fusion.8 = f32[512,512]{1,0:T(8,128)} fusion(bf16[192,512]{1,0:T(8,128)(2,1)S(1)} %get-tuple-element.30, bf16[192,512]{1,0:T(8,128)(2,1)S(1)} %get-tuple-element.27, bf16[192,512]{1,0:T(8,128)(2,1)S(1)} %get-tuple-element.26, bf16[192,512]{1,0:T(8,128)(2,1)S(1)} %get-tuple-element.25), kind=kOutput, calls=%fused_computation.9 | convolution fusion | flops 202899456 | bytes 1835008 | tf_op jit(solution)/shard_map/dot_general | solution.py:26
  101.8 1.4 %fusion.4 = f32[512,512]{1,0:T(8,128)} fusion(bf16[384,512]{1,0:T(8,128)(2,1)S(1)} %constant_dynamic-update-slice_fusion, bf16[192,512]{1,0:T(8,128)(2,1)S(1)} %get-tuple-element.31, bf16[192,512]{1,0:T(8,128)(2,1)S(1)} %get-tuple-element.28), kind=kOutput, calls=%fused_computation.5 | convolution fusion | flops 202113024 | bytes 1835008 | tf_op jit(solution)/shard_map/dot_general | solution.py:26
  103.3 1.4 %fusion = f32[512,512]{1,0:T(8,128)} fusion(bf16[384,512]{1,0:T(8,128)(2,1)S(1)} %constant_dynamic-update-slice_fusion, bf16[192,512]{1,0:T(8,128)(2,1)S(1)} %get-tuple-element.32, bf16[192,512]{1,0:T(8,128)(2,1)S(1)} %get-tuple-element.29), kind=kOutput, calls=%fused_computation.1 | convolution fusion | flops 202113024 | bytes 1835008 | tf_op jit(solution)/shard_map/dot_general | solution.py:26
  104.7 18.8 %all-to-all-done.4.blocks = bf16[32,24,512]{2,1,0:T(8,128)(2,1)S(1)} async-done(((bf16[32,24,512]{2,1,0:T(8,128)(2,1)}), bf16[32,24,512]{2,1,0:T(8,128)(2,1)S(1)}, u32[]{:S(2)}, u32[]{:S(2)}) %all-to-all-start.4) | async-done | bytes 786464 | tf_op jit(solution)/shard_map/all_to_all | solution.py:178
  123.5 0.7 totals.1
  (14 shorter events, 0.2 us)
Async XLA Ops:
  0.6 0.7 copy-start.3
  1.4 0.7 copy-start.4
  18.6 14.3 %copy-start = (bf16[512,512]{1,0:T(8,128)(2,1)S(1)}, bf16[512,512]{1,0:T(8,128)(2,1)}, u32[]{:S(2)}) copy-start(bf16[512,512]{1,0:T(8,128)(2,1)} %gate_weight.5) | copy-start | bytes 1572868
  18.6 14.3 %copy-start.1 = (bf16[512,512]{1,0:T(8,128)(2,1)S(1)}, bf16[512,512]{1,0:T(8,128)(2,1)}, u32[]{:S(2)}) copy-start(bf16[512,512]{1,0:T(8,128)(2,1)} %up_weight.5) | copy-start | bytes 1572868
  18.6 14.3 %copy-start.2 = (bf16[512,512]{1,0:T(8,128)(2,1)S(1)}, bf16[512,512]{1,0:T(8,128)(2,1)}, u32[]{:S(2)}) copy-start(bf16[512,512]{1,0:T(8,128)(2,1)} %down_weight.5) | copy-start | bytes 1572868
  33.5 4.7 %collective-permute-start = (f32[192,1536]{1,0:T(8,128)S(1)}, f32[192,1536]{1,0:T(8,128)S(1)}, u32[]{:S(2)}, u32[]{:S(2)}) collective-permute-start(f32[192,1536]{1,0:T(8,128)S(1)} %get-tuple-element.20), channel_id=1, source_target_pairs={{0,1},{1,0},{2,3},{3,2},{4,5},{5,4},{6,7},{7,6},{8,9},{9,8},{10,11... | collective-permute-start | bytes 3538952 | tf_op jit(solution)/shard_map/ppermute | solution.py:162
  88.6 3.9 %collective-permute-start.1 = (bf16[192,1536]{1,0:T(8,128)(2,1)S(1)}, bf16[192,1536]{1,0:T(8,128)(2,1)S(1)}, u32[]{:S(2)}, u32[]{:S(2)}) collective-permute-start(bf16[192,1536]{1,0:T(8,128)(2,1)S(1)} %bitcast.10), channel_id=1, source_target_pairs={{0,1},{1,0},{2,3},{3,2},{4,5},{5,4},{6,7},{7,6},{8,9},{9,8},{10,11... | collective-permute-start | bytes 1769480 | tf_op jit(solution)/shard_map/ppermute | solution.py:176
  94.5 29.1 %all-to-all-start.4 = ((bf16[32,24,512]{2,1,0:T(8,128)(2,1)}), bf16[32,24,512]{2,1,0:T(8,128)(2,1)S(1)}, u32[]{:S(2)}, u32[]{:S(2)}) async-start(bf16[32,24,512]{2,1,0:T(8,128)(2,1)} %output_blocks.1), calls=%async_computation.4 | async-start | bytes 1572864 | tf_op jit(solution)/shard_map/all_to_all | solution.py:178

commit v2 on v1

--- a/solution.py
+++ b/solution.py
@@ -41,24 +41,27 @@
     return lax.broadcasted_iota(jnp.int32, shape, 1) < 4
 
 
-def pack_kernel(a, b, out):
-    head = (a[:8], b[:8])
-    tail = jnp.concatenate([a[8:].astype(F32), b[8:].astype(F32)], axis=0).astype(BF16)
+def pack_kernel(both, out):
+    first, middle, last = (both[i : i + 8].astype(F32) for i in (0, 8, 16))
+    low = lax.broadcasted_iota(jnp.int32, first.shape, 0) < 4
+    second = jnp.where(low, pltpu.roll(middle, 4, 0), pltpu.roll(last, 4, 0))
+    tail = jnp.where(low, middle, last)
     for i in range(out.shape[0]):
-        out[i, 0:8, :] = head[0]
-        out[i, 8:16, :] = head[1]
-        out[i, 16:24, :] = tail
+        out[i, 0:8, :] = first.astype(BF16)
+        out[i, 8:16, :] = second.astype(BF16)
+        out[i, 16:24, :] = tail.astype(BF16)
 
 
 def pack(a, b, copies):
+    both = jnp.concatenate([a, b], axis=0)
     return pl.pallas_call(
         pack_kernel,
-        out_shape=jax.ShapeDtypeStruct((copies, 24, a.shape[1]), BF16),
-        in_specs=[VM, VM],
+        out_shape=jax.ShapeDtypeStruct((copies,) + both.shape, BF16),
+        in_specs=[VM],
         out_specs=VM,
         compiler_params=PARAMS,
         name="pack",
-    )(a, b)
+    )(both)
 
 
 def total_kernel(blocks, layer_out, input_grad):
@@ -113,36 +116,42 @@
     )(which, blocks, gate_weight, up_weight, down_weight)
 
 
-def output_kernel(which, own, other, gate_weight, up_weight, down_weight, out):
+def output_kernel(which, part, gate_weight, up_weight, down_weight, *rest):
+    out = rest[-1]
     h = gate_weight.shape[1]
     d = gate_weight.shape[0]
-    for part, where in ((own, which[0]), (other, 1 - which[0])):
-        m = part.shape[0] // 12
-        f = mm(part[:, :h], down_weight[...])
-        b = mm_t(part[:, h : 2 * h], gate_weight[...]) + mm_t(part[:, 2 * h :], up_weight[...])
-        rows = pl.ds(where * m, m)
-        out[rows, 0:8, :] = f[: m * 8].reshape(m, 8, d).astype(BF16)
-        out[rows, 8:16, :] = b[: m * 8].reshape(m, 8, d).astype(BF16)
-        f = f[m * 8 :].reshape(m // 2, 8, d)
-        b = b[m * 8 :].reshape(m // 2, 8, d)
-        low = low_rows(f.shape)
-        even = jnp.where(low, f, pltpu.roll(b, 4, 1))
-        odd = jnp.where(low, pltpu.roll(f, 4, 1), b)
-        out[rows, 16:24, :] = jnp.concatenate([even, odd], axis=1).reshape(m, 8, d).astype(BF16)
-
-
-def output_blocks(which, own, other, gate_weight, up_weight, down_weight):
-    n, width = own.shape
-    d = gate_weight.shape[0]
+    m = out.shape[0]
+    f = mm(part[:, :h], down_weight[...])
+    b = mm_t(part[:, h : 2 * h], gate_weight[...]) + mm_t(part[:, 2 * h :], up_weight[...])
+    out[:, 0:8, :] = f[: m * 8].reshape(m, 8, d).astype(BF16)
+    out[:, 8:16, :] = b[: m * 8].reshape(m, 8, d).astype(BF16)
+    f = f[m * 8 :].reshape(m // 2, 8, d)
+    b = b[m * 8 :].reshape(m // 2, 8, d)
+    low = low_rows(f.shape)
+    even = jnp.where(low, f, pltpu.roll(b, 4, 1))
+    odd = jnp.where(low, pltpu.roll(f, 4, 1), b)
+    out[:, 16:24, :] = jnp.concatenate([even, odd], axis=1).reshape(m, 8, d).astype(BF16)
+
+
+def output_blocks(which, part, weights, blocks=None):
+    n, width = part.shape
+    d = weights[0].shape[0]
+    m = n // 12
+    more = [] if blocks is None else [blocks]
     return pl.pallas_call(
         output_kernel,
-        out_shape=jax.ShapeDtypeStruct((n // 6, 24, d), BF16),
-        in_specs=[SM, VM, VM, VM, VM, VM],
-        out_specs=VM,
+        out_shape=jax.ShapeDtypeStruct((2 * m, 24, d), BF16),
+        grid_spec=pltpu.PrefetchScalarGridSpec(
+            num_scalar_prefetch=1,
+            grid=(1,),
+            in_specs=[VM, VM, VM, VM] + [pl.BlockSpec(memory_space=pl.ANY)] * len(more),
+            out_specs=pl.BlockSpec((m, 24, d), lambda i, which: (which[0], 0, 0)),
+        ),
+        input_output_aliases={5: 0} if more else {},
         compiler_params=PARAMS,
-        cost_estimate=pl.CostEstimate(flops=4 * n * d * width, bytes_accessed=8 * n * d, transcendentals=0),
+        cost_estimate=pl.CostEstimate(flops=2 * n * d * width, bytes_accessed=4 * n * d, transcendentals=0),
         name="output_blocks",
-    )(which, own, other, gate_weight, up_weight, down_weight)
+    )(which, part, *weights, *more)
 
 
 def local(sizes, activations, gate_weight, up_weight, down_weight, out_grad):
@@ -174,7 +183,8 @@
     mine = jnp.concatenate([hidden, gate_delta, up_delta], axis=1)
     own = spread(mine, "z", nz).reshape(half, 3 * h)
     other = lax.ppermute(own, "core", swap)
-    blocks = output_blocks(core, own, other, *weights)
+    blocks = output_blocks(core, own, weights)
+    blocks = output_blocks(away, other, weights, blocks)
     layer_out, input_grad = totals(lax.all_to_all(blocks, ("x", "y"), 0, 0))
 
     hid, gd, ud = (jnp.concatenate([own[:, i * h : (i + 1) * h], other[:, i * h : (i + 1) * h]], axis=0) for i in range(3))

time: 125 us -> 123 us (0.984)
  local copies, waits for them, and re-layouts: 1.65 us -> 0.22 us
  waiting for transfers between devices: 23.1 us -> 21.7 us
    unnamed x11 -> x7, local copies, waits for them, and re-layouts: 1.45 us -> 0.03 us
    ppermute x1, waiting for transfers between devices: 1.97 us -> 0.61 us  [local(): other = lax.ppermute(own, 'core', swap)]
    pallas_call x2 -> x3, Pallas kernels: 1.98 us -> 2.73 us  [the longest x2 2.72 us: output_blocks(): pl.pallas_call(output_kernel, out_shape=jax.ShapeDtypeStruct((2 * m, 24,...]
  transfers between devices with their start and end apart: 3 -> 3, of which waited for: 3 -> 3; matrix products, arithmetic and copies ran while one was open for 4% -> 4% of each run, Pallas kernels for 0% -> 2%
where the time goes in v2:
time: 123 us
  blocking collectives  80.8 us (66%)
  waiting for transfers between devices  21.7 us (18%)
  starting transfers between devices  9.6 us (8%)
  Pallas kernels  4.54 us (4%)
  matrix products  4.31 us (4%)
    all_to_all x2, blocking collectives, spread(): lax.all_to_all(jnp.broadcast_to(block[None], (size,) + block.shape), axis...  35 us
    all_to_all x1, blocking collectives, local(): summed = add_up(lax.all_to_all(chip, 'z', 0, 0))  29.3 us
    all_to_all x1, waiting for transfers between devices, local(): layer_out, input_grad = totals(lax.all_to_all(blocks, ('x', 'y'), 0, 0))  18.8 us
    all_to_all x1, blocking collectives, local(): both = spread(lax.all_to_all(both, 'y', 0, 0), 'x', nx).reshape(rows, 24, d)  16.5 us
    all_to_all x1, starting transfers between devices, local(): layer_out, input_grad = totals(lax.all_to_all(blocks, ('x', 'y'), 0, 0))  5.77 us
    dot_general x3, matrix products, t_mm(): lax.dot_general(left, right, (((0,), (0,)), ((), ())), preferred_element_...  4.31 us
    pallas_call x2, Pallas kernels, output_blocks(): pl.pallas_call(output_kernel, out_shape=jax.ShapeDtypeStruct((2 * m, 24,...  2.72 us
  transfers between devices with their start and end apart: 3, of which 3 were waited for; matrix products, arithmetic and copies ran while one was open for 4% of the time, Pallas kernels for 2%

profile of v2, /device:TPU:8, one launch (start us, length us, event | category | flops | bytes accessed | tf_op | source)
XLA Modules:
  0.0 123.0 jit_solution(10798294602677888168)
XLA Ops:
  0.6 0.7 pad_maximum_fusion.1.both
  1.4 16.5 %all_to_all.25 = bf16[8,24,512]{2,1,0:T(8,128)(2,1)S(1)} all-to-all(bf16[8,24,512]{2,1,0:T(8,128)(2,1)S(1)} %pack.1), channel_id=1, replica_groups=mesh['y'=8,'x'=4,'z'=8,'core'=2] {'y'}, dimensions={0} | all-to-all | bytes 393216 | tf_op jit(solution)/shard_map/all_to_all | solution.py:168
  18.0 0.1 broadcast_in_dim.4
  18.0 14.2 %all_to_all.26 = bf16[4,8,24,512]{3,2,1,0:T(8,128)(2,1)S(1)} all-to-all(bf16[4,8,24,512]{3,2,1,0:T(8,128)(2,1)S(1)} %broadcast_in_dim.4), channel_id=1, replica_groups=mesh['y'=8,'x'=4,'z'=8,'core'=2] {'x'}, dimensions={0} | all-to-all | bytes 1572864 | tf_op jit(solution)/shard_map/all_to_all | solution.py:30
  32.2 0.0 copy-done
  32.2 0.0 copy-done.2
  32.2 0.5 partial_sums.3
  32.8 1.9 %collective-permute-start = (f32[192,1536]{1,0:T(8,128)S(1)}, f32[192,1536]{1,0:T(8,128)S(1)}, u32[]{:S(2)}, u32[]{:S(2)}) collective-permute-start(f32[192,1536]{1,0:T(8,128)S(1)} %get-tuple-element.20), channel_id=1, source_target_pairs={{0,1},{1,0},{2,3},{3,2},{4,5},{5,4},{6,7},{7,6},{8,9},{9,8},{10,11... | collective-permute-start | bytes 3538952 | tf_op jit(solution)/shard_map/ppermute | solution.py:171
  34.7 0.5 partial_sums.2
  35.3 2.3 %collective-permute-done = f32[192,1536]{1,0:T(8,128)S(1)} collective-permute-done((f32[192,1536]{1,0:T(8,128)S(1)}, f32[192,1536]{1,0:T(8,128)S(1)}, u32[]{:S(2)}, u32[]{:S(2)}) %collective-permute-start) | collective-permute-done | bytes 1179680 | tf_op jit(solution)/shard_map/ppermute | solution.py:171
  37.5 0.1 add_convert_fusion
  37.7 29.3 %all_to_all.27 = bf16[8,24,1536]{2,1,0:T(8,128)(2,1)S(1)} all-to-all(bf16[8,24,1536]{2,1,0:T(8,128)(2,1)S(1)} %bitcast.13), channel_id=1, replica_groups=mesh['y'=8,'x'=4,'z'=8,'core'=2] {'z'}, dimensions={0} | all-to-all | bytes 1179648 | tf_op jit(solution)/shard_map/all_to_all | solution.py:176
  67.0 0.1 add_bitcast_fusion
  67.2 20.8 %all_to_all.28 = bf16[8,24,1536]{2,1,0:T(8,128)(2,1)S(1)} all-to-all(bf16[8,24,1536]{2,1,0:T(8,128)(2,1)S(1)} %broadcast_in_dim.5), channel_id=1, replica_groups=mesh['y'=8,'x'=4,'z'=8,'core'=2] {'z'}, dimensions={0} | all-to-all | bytes 1179648 | tf_op jit(solution)/shard_map/all_to_all | solution.py:30
  87.9 1.9 %collective-permute-start.1 = (bf16[192,1536]{1,0:T(8,128)(2,1)S(1)}, bf16[192,1536]{1,0:T(8,128)(2,1)S(1)}, u32[]{:S(2)}, u32[]{:S(2)}) collective-permute-start(bf16[192,1536]{1,0:T(8,128)(2,1)S(1)} %bitcast.10), channel_id=1, source_target_pairs={{0,1},{1,0},{2,3},{3,2},{4,5},{5,4},{6,7},{7,6},{8,9},{9,8},{10,11... | collective-permute-start | bytes 1769480 | tf_op jit(solution)/shard_map/ppermute | solution.py:185
  89.9 1.4 %output_blocks.2.rest_0_ = bf16[32,24,512]{2,1,0:T(8,128)(2,1)} custom-call(s32[1]{0:T(128)} %bitcast.which, bf16[192,1536]{1,0:T(8,128)(2,1)S(1)} %bitcast.11, bf16[512,512]{1,0:T(8,128)(2,1)S(1)} %copy-done, bf16[512,512]{1,0:T(8,128)(2,1)S(1)} %copy-done.1, bf16[512,512]{1,0:T(8,128)(2,1)S(1)} %copy-done.2), custom_call_target="tpu_custom_call" | custom-call | flops 301989888 | bytes 393216 | tf_op jit(solution)/shard_map/output_blocks/pallas_call | solution.py:141
  91.2 0.6 collective-permute-done.1.part
  91.8 1.4 %output_blocks.3 = bf16[32,24,512]{2,1,0:T(8,128)(2,1)} custom-call(s32[1]{0:T(128)S(6)} %sub.6.which, bf16[192,1536]{1,0:T(8,128)(2,1)S(1)} %collective-permute-done.1.part, bf16[512,512]{1,0:T(8,128)(2,1)S(1)} %copy-done, bf16[512,512]{1,0:T(8,128)(2,1)S(1)} %copy-done.1, bf16[512,512]{1,0:T(8,128)(2,1)S(1)} %copy-done.2, ...), custom_call_target="tpu_custom_call", output_to_operand_aliasing={{}: (5, {})} | custom-call | flops 301989888 | bytes 393216 | tf_op jit(solution)/shard_map/output_blocks/pallas_call | solution.py:141
  93.2 5.8 %all-to-all-start.4 = ((bf16[32,24,512]{2,1,0:T(8,128)(2,1)}), bf16[32,24,512]{2,1,0:T(8,128)(2,1)S(1)}, u32[]{:S(2)}, u32[]{:S(2)}) async-start(bf16[32,24,512]{2,1,0:T(8,128)(2,1)} %output_blocks.3), calls=%async_computation.4 | async-start | bytes 1572864 | tf_op jit(solution)/shard_map/all_to_all | solution.py:188
  99.1 1.4 %fusion.8 = f32[512,512]{1,0:T(8,128)} fusion(bf16[192,512]{1,0:T(8,128)(2,1)S(1)} %get-tuple-element.30, bf16[192,512]{1,0:T(8,128)(2,1)S(1)} %get-tuple-element.27, bf16[192,512]{1,0:T(8,128)(2,1)S(1)} %get-tuple-element.26, bf16[192,512]{1,0:T(8,128)(2,1)S(1)} %get-tuple-element.25), kind=kOutput, calls=%fused_computation.9 | convolution fusion | flops 202899456 | bytes 1835008 | tf_op jit(solution)/shard_map/dot_general | solution.py:26
  100.6 1.4 %fusion = f32[512,512]{1,0:T(8,128)} fusion(bf16[384,512]{1,0:T(8,128)(2,1)S(1)} %constant_dynamic-update-slice_fusion, bf16[192,512]{1,0:T(8,128)(2,1)S(1)} %get-tuple-element.32, bf16[192,512]{1,0:T(8,128)(2,1)S(1)} %get-tuple-element.29), kind=kOutput, calls=%fused_computation.1 | convolution fusion | flops 202113024 | bytes 1835008 | tf_op jit(solution)/shard_map/dot_general | solution.py:26
  102.0 1.4 %fusion.4 = f32[512,512]{1,0:T(8,128)} fusion(bf16[384,512]{1,0:T(8,128)(2,1)S(1)} %constant_dynamic-update-slice_fusion, bf16[192,512]{1,0:T(8,128)(2,1)S(1)} %get-tuple-element.31, bf16[192,512]{1,0:T(8,128)(2,1)S(1)} %get-tuple-element.28), kind=kOutput, calls=%fused_computation.5 | convolution fusion | flops 202113024 | bytes 1835008 | tf_op jit(solution)/shard_map/dot_general | solution.py:26
  103.4 18.8 %all-to-all-done.4.blocks = bf16[32,24,512]{2,1,0:T(8,128)(2,1)S(1)} async-done(((bf16[32,24,512]{2,1,0:T(8,128)(2,1)}), bf16[32,24,512]{2,1,0:T(8,128)(2,1)S(1)}, u32[]{:S(2)}, u32[]{:S(2)}) %all-to-all-start.4) | async-done | bytes 786464 | tf_op jit(solution)/shard_map/all_to_all | solution.py:188
  122.3 0.7 totals.1
  (12 shorter events, 0.2 us)
Async XLA Ops:
  18.0 14.3 %copy-start = (bf16[512,512]{1,0:T(8,128)(2,1)S(1)}, bf16[512,512]{1,0:T(8,128)(2,1)}, u32[]{:S(2)}) copy-start(bf16[512,512]{1,0:T(8,128)(2,1)} %gate_weight.7) | copy-start | bytes 1572868
  18.0 14.3 %copy-start.1 = (bf16[512,512]{1,0:T(8,128)(2,1)S(1)}, bf16[512,512]{1,0:T(8,128)(2,1)}, u32[]{:S(2)}) copy-start(bf16[512,512]{1,0:T(8,128)(2,1)} %up_weight.7) | copy-start | bytes 1572868
  18.0 14.3 %copy-start.2 = (bf16[512,512]{1,0:T(8,128)(2,1)S(1)}, bf16[512,512]{1,0:T(8,128)(2,1)}, u32[]{:S(2)}) copy-start(bf16[512,512]{1,0:T(8,128)(2,1)} %down_weight.7) | copy-start | bytes 1572868
  32.8 4.7 %collective-permute-start = (f32[192,1536]{1,0:T(8,128)S(1)}, f32[192,1536]{1,0:T(8,128)S(1)}, u32[]{:S(2)}, u32[]{:S(2)}) collective-permute-start(f32[192,1536]{1,0:T(8,128)S(1)} %get-tuple-element.20), channel_id=1, source_target_pairs={{0,1},{1,0},{2,3},{3,2},{4,5},{5,4},{6,7},{7,6},{8,9},{9,8},{10,11... | collective-permute-start | bytes 3538952 | tf_op jit(solution)/shard_map/ppermute | solution.py:171
  87.9 3.9 %collective-permute-start.1 = (bf16[192,1536]{1,0:T(8,128)(2,1)S(1)}, bf16[192,1536]{1,0:T(8,128)(2,1)S(1)}, u32[]{:S(2)}, u32[]{:S(2)}) collective-permute-start(bf16[192,1536]{1,0:T(8,128)(2,1)S(1)} %bitcast.10), channel_id=1, source_target_pairs={{0,1},{1,0},{2,3},{3,2},{4,5},{5,4},{6,7},{7,6},{8,9},{9,8},{10,11... | collective-permute-start | bytes 1769480 | tf_op jit(solution)/shard_map/ppermute | solution.py:185
  93.2 29.1 %all-to-all-start.4 = ((bf16[32,24,512]{2,1,0:T(8,128)(2,1)}), bf16[32,24,512]{2,1,0:T(8,128)(2,1)S(1)}, u32[]{:S(2)}, u32[]{:S(2)}) async-start(bf16[32,24,512]{2,1,0:T(8,128)(2,1)} %output_blocks.3), calls=%async_computation.4 | async-start | bytes 1572864 | tf_op jit(solution)/shard_map/all_to_all | solution.py:188

commit v3 on v2

--- a/solution.py
+++ b/solution.py
@@ -79,41 +79,67 @@
     return pl.pallas_call(total_kernel, out_shape=(shape, shape), in_specs=[VM], compiler_params=PARAMS, name="totals")(blocks)
 
 
-def partial_kernel(which, blocks, gate_weight, up_weight, down_weight, out, x_out, g_out):
-    m = x_out.shape[0] // 12
-    d = x_out.shape[1]
-    rows = pl.ds(which[0] * m, m)
+def unpack(blocks, rows):
+    m, d = rows.size, blocks.shape[2]
     tail = blocks[rows, 16:24, :].astype(F32).reshape(m // 2, 16, d)
     even, odd = tail[:, :8], tail[:, 8:]
     low = low_rows(even.shape)
-    x_tail = jnp.where(low, even, pltpu.roll(odd, 4, 1)).reshape(m * 4, d)
-    g_tail = jnp.where(low, pltpu.roll(even, 4, 1), odd).reshape(m * 4, d)
-    x_head = blocks[rows, 0:8, :].astype(F32).reshape(m * 8, d)
-    g_head = blocks[rows, 8:16, :].astype(F32).reshape(m * 8, d)
-    x = jnp.concatenate([x_head, x_tail], axis=0).astype(BF16)
-    g = jnp.concatenate([g_head, g_tail], axis=0).astype(BF16)
-    x_out[...] = x
-    g_out[...] = g
-    h = gate_weight.shape[1]
+    a_tail = jnp.where(low, even, pltpu.roll(odd, 4, 1)).reshape(m * 4, d)
+    b_tail = jnp.where(low, pltpu.roll(even, 4, 1), odd).reshape(m * 4, d)
+    a_head = blocks[rows, 0:8, :].astype(F32).reshape(m * 8, d)
+    b_head = blocks[rows, 8:16, :].astype(F32).reshape(m * 8, d)
+    a = jnp.concatenate([a_head, a_tail], axis=0).astype(BF16)
+    b = jnp.concatenate([b_head, b_tail], axis=0).astype(BF16)
+    return a, b
+
+
+def near_kernel(which, blocks, gate_weight, up_weight, down_weight, out, x_all, g_all):
+    m = blocks.shape[0] // 2
+    n = x_all.shape[0] // 2
+    h = gate_weight.shape[1]
+    x, g = unpack(blocks, pl.ds(which[0] * m, m))
+    x_all[:n], g_all[:n] = x, g
     out[:, :h] = mm(x, gate_weight[...])
     out[:, h : 2 * h] = mm(x, up_weight[...])
     out[:, 2 * h :] = mm_t(g, down_weight[...])
-
-
-def partial_sums(which, blocks, gate_weight, up_weight, down_weight):
-    n = blocks.shape[0] * 12 // 2
+    x_all[n:], g_all[n:] = unpack(blocks, pl.ds((1 - which[0]) * m, m))
+
+
+def near_sums(which, blocks, weights):
+    n = blocks.shape[0] * 12
     d = blocks.shape[2]
-    h = gate_weight.shape[1]
+    h = weights[0].shape[1]
     shape = jax.ShapeDtypeStruct
     return pl.pallas_call(
-        partial_kernel,
-        out_shape=(shape((n, 3 * h), F32), shape((n, d), BF16), shape((n, d), BF16)),
+        near_kernel,
+        out_shape=(shape((n // 2, 3 * h), F32), shape((n, d), BF16), shape((n, d), BF16)),
         in_specs=[SM, VM, VM, VM, VM],
         out_specs=(VM, VM, VM),
         compiler_params=PARAMS,
-        cost_estimate=pl.CostEstimate(flops=2 * n * d * 3 * h, bytes_accessed=4 * n * 3 * h, transcendentals=0),
-        name="partial_sums",
-    )(which, blocks, gate_weight, up_weight, down_weight)
+        cost_estimate=pl.CostEstimate(flops=3 * n * d * h, bytes_accessed=6 * n * h, transcendentals=0),
+        name="near_sums",
+    )(which, blocks, *weights)
+
+
+def far_kernel(near, blocks, gate_weight, up_weight, down_weight, out):
+    h = gate_weight.shape[1]
+    x, g = unpack(blocks, pl.ds(0, blocks.shape[0]))
+    out[:, :h] = (near[:, :h] + mm(x, gate_weight[...])).astype(BF16)
+    out[:, h : 2 * h] = (near[:, h : 2 * h] + mm(x, up_weight[...])).astype(BF16)
+    out[:, 2 * h :] = (near[:, 2 * h :] + mm_t(g, down_weight[...])).astype(BF16)
+
+
+def far_sums(near, blocks, weights):
+    n, width = near.shape
+    return pl.pallas_call(
+        far_kernel,
+        out_shape=jax.ShapeDtypeStruct(near.shape, BF16),
+        in_specs=[VM, VM, VM, VM, VM],
+        out_specs=VM,
+        compiler_params=PARAMS,
+        cost_estimate=pl.CostEstimate(flops=2 * n * width * blocks.shape[2], bytes_accessed=6 * n * width, transcendentals=0),
+        name="far_sums",
+    )(near, blocks, *weights)
 
 
 def output_kernel(which, part, gate_weight, up_weight, down_weight, *rest):
@@ -165,14 +191,17 @@
 
     both = pack(activations, out_grad, ny)
     both, core, away = lax.optimization_barrier((both, core, away))
-    both = spread(lax.all_to_all(both, "y", 0, 0), "x", nx).reshape(rows, 24, d)
     weights = (gate_weight, up_weight, down_weight)
-    send, x_other, g_other = partial_sums(away, both, *weights)
-    sent = lax.ppermute(send, "core", swap)
-    keep, x_own, g_own = partial_sums(core, both, *weights)
-    half = keep.shape[0]
+    column = lax.all_to_all(both, "y", 0, 0)
+    column, *moving = lax.optimization_barrier((column, *weights))
+    far_weights = [lax.ppermute(w, "core", swap) for w in moving]
+    both = spread(column, "x", nx).reshape(rows, 24, d)
+    theirs = lax.dynamic_slice_in_dim(both, away[0] * (rows // nc), rows // nc, axis=0)
+    far = lax.ppermute(theirs, "core", swap)
+    near, x_cat, g_cat = near_sums(core, both, weights)
+    half = near.shape[0]
     n = half // nz
-    chip = (keep + sent).astype(BF16).reshape(nz, n, 3 * h)
+    chip = far_sums(near, far, far_weights).reshape(nz, n, 3 * h)
     summed = add_up(lax.all_to_all(chip, "z", 0, 0))
     gate, up, hidden_grad = summed[:, :h], summed[:, h : 2 * h], summed[:, 2 * h :]
     sig = jax.nn.sigmoid(gate)
@@ -188,8 +217,6 @@
     layer_out, input_grad = totals(lax.all_to_all(blocks, ("x", "y"), 0, 0))
 
     hid, gd, ud = (jnp.concatenate([own[:, i * h : (i + 1) * h], other[:, i * h : (i + 1) * h]], axis=0) for i in range(3))
-    x_cat = jnp.concatenate([x_own, x_other], axis=0)
-    g_cat = jnp.concatenate([g_own, g_other], axis=0)
     return layer_out, input_grad, t_mm(x_cat, gd), t_mm(x_cat, ud), t_mm(hid, g_cat)
 
 

time: 123 us -> 124 us (level)
  blocking collectives: 80.8 us -> 66.6 us
  starting transfers between devices: 9.6 us -> 20 us
  waiting for transfers between devices: 21.7 us -> 24.5 us
    all_to_all x2 -> x1, blocking collectives: 35 us -> 20.8 us  [spread(): lax.all_to_all(jnp.broadcast_to(block[None], (size,) + block.shape), axis...]
    ppermute x1 -> x4, starting transfers between devices: 1.92 us -> 8.16 us  [the longest x3 6.24 us: local(): far_weights = [lax.ppermute(w, 'core', swap) for w in moving]]
    all_to_all x0 -> x1, starting transfers between devices: none -> 4.11 us  [spread(): lax.all_to_all(jnp.broadcast_to(block[None], (size,) + block.shape), axis...]
    all_to_all x0 -> x1, waiting for transfers between devices: none -> 3.88 us  [spread(): lax.all_to_all(jnp.broadcast_to(block[None], (size,) + block.shape), axis...]
  transfers between devices with their start and end apart: 3 -> 7, of which waited for: 3 -> 4; matrix products, arithmetic and copies ran while one was open for 4% -> 4% of each run, Pallas kernels for 2% -> 2%
where the time goes in v3:
time: 124 us
  blocking collectives  66.6 us (54%)
  waiting for transfers between devices  24.5 us (20%)
  starting transfers between devices  20 us (16%)
  Pallas kernels  5.76 us (5%)
  matrix products  4.29 us (3%)
    all_to_all x1, blocking collectives, local(): summed = add_up(lax.all_to_all(chip, 'z', 0, 0))  29.3 us
    all_to_all x1, blocking collectives, spread(): lax.all_to_all(jnp.broadcast_to(block[None], (size,) + block.shape), axis...  20.8 us
    all_to_all x1, waiting for transfers between devices, local(): layer_out, input_grad = totals(lax.all_to_all(blocks, ('x', 'y'), 0, 0))  18.9 us
    all_to_all x1, blocking collectives, local(): column = lax.all_to_all(both, 'y', 0, 0)  16.5 us
    ppermute x3, starting transfers between devices, local(): far_weights = [lax.ppermute(w, 'core', swap) for w in moving]  6.24 us
    all_to_all x1, starting transfers between devices, local(): layer_out, input_grad = totals(lax.all_to_all(blocks, ('x', 'y'), 0, 0))  5.78 us
    dot_general x3, matrix products, t_mm(): lax.dot_general(left, right, (((0,), (0,)), ((), ())), preferred_element_...  4.29 us
    all_to_all x1, starting transfers between devices, spread(): lax.all_to_all(jnp.broadcast_to(block[None], (size,) + block.shape), axis...  4.11 us
  transfers between devices with their start and end apart: 7, of which 4 were waited for; matrix products, arithmetic and copies ran while one was open for 4% of the time, Pallas kernels for 2%

profile of v3, /device:TPU:8, one launch (start us, length us, event | category | flops | bytes accessed | tf_op | source)
XLA Modules:
  0.0 123.9 jit_solution(13462304811168334545)
XLA Ops:
  0.6 0.7 pad_maximum_fusion.1.both
  1.4 16.5 %all_to_all.25 = bf16[8,24,512]{2,1,0:T(8,128)(2,1)S(1)} all-to-all(bf16[8,24,512]{2,1,0:T(8,128)(2,1)S(1)} %pack.1), channel_id=1, replica_groups=mesh['y'=8,'x'=4,'z'=8,'core'=2] {'y'}, dimensions={0} | all-to-all | bytes 393216 | tf_op jit(solution)/shard_map/all_to_all | solution.py:195
  18.0 0.9 broadcast_in_dim.4
  18.9 4.1 %all-to-all-start.1 = ((bf16[4,8,24,512]{3,2,1,0:T(8,128)(2,1)}), bf16[4,8,24,512]{3,2,1,0:T(8,128)(2,1)S(1)}, u32[]{:S(2)}, u32[]{:S(2)}) async-start(bf16[4,8,24,512]{3,2,1,0:T(8,128)(2,1)} %broadcast_in_dim.4), calls=%async_computation.1 | async-start | bytes 1572864 | tf_op jit(solution)/shard_map/all_to_all | solution.py:30
  23.0 1.9 %collective-permute-start.1 = (bf16[512,512]{1,0:T(8,128)(2,1)S(1)}, bf16[512,512]{1,0:T(8,128)(2,1)S(1)}, u32[]{:S(2)}, u32[]{:S(2)}) collective-permute-start(bf16[512,512]{1,0:T(8,128)(2,1)S(1)} %copy-done), channel_id=1, source_target_pairs={{0,1},{1,0},{2,3},{3,2},{4,5},{5,4},{6,7},{7,6},{8,9},{9,8},{10,11... | collective-permute-start | bytes 1572872 | tf_op jit(solution)/shard_map/ppermute | solution.py:197
  24.9 2.4 %collective-permute-start.2 = (bf16[512,512]{1,0:T(8,128)(2,1)S(1)}, bf16[512,512]{1,0:T(8,128)(2,1)}, u32[]{:S(2)}, u32[]{:S(2)}) collective-permute-start(bf16[512,512]{1,0:T(8,128)(2,1)S(1)} %copy-done.1), channel_id=1, source_target_pairs={{0,1},{1,0},{2,3},{3,2},{4,5},{5,4},{6,7},{7,6},{8,9},{9,8},{10,11... | collective-permute-start | bytes 1572872 | tf_op jit(solution)/shard_map/ppermute | solution.py:197
  27.4 1.9 %collective-permute-start.3 = (bf16[512,512]{1,0:T(8,128)(2,1)S(1)}, bf16[512,512]{1,0:T(8,128)(2,1)}, u32[]{:S(2)}, u32[]{:S(2)}) collective-permute-start(bf16[512,512]{1,0:T(8,128)(2,1)S(1)} %copy-done.2), channel_id=1, source_target_pairs={{0,1},{1,0},{2,3},{3,2},{4,5},{5,4},{6,7},{7,6},{8,9},{9,8},{10,11... | collective-permute-start | bytes 1572872 | tf_op jit(solution)/shard_map/ppermute | solution.py:197
  29.3 3.9 %all-to-all-done.1 = bf16[4,8,24,512]{3,2,1,0:T(8,128)(2,1)S(1)} async-done(((bf16[4,8,24,512]{3,2,1,0:T(8,128)(2,1)}), bf16[4,8,24,512]{3,2,1,0:T(8,128)(2,1)S(1)}, u32[]{:S(2)}, u32[]{:S(2)}) %all-to-all-start.1) | async-done | bytes 786464 | tf_op jit(solution)/shard_map/all_to_all | solution.py:30
  33.2 1.9 %collective-permute-start = (bf16[16,24,512]{2,1,0:T(8,128)(2,1)S(1)}, bf16[16,24,512]{2,1,0:T(8,128)(2,1)S(1)}, u32[]{:S(2)}, u32[]{:S(2)}) collective-permute-start(bf16[16,24,512]{2,1,0:T(8,128)(2,1)S(1)} %constant_dynamic-slice_fusion), channel_id=1, source_target_pairs={{0,1},{1,0},{2,3},{3,2},{4,5},{5,4},{6,7},{7,6},{8,9},{9,8},{10,11... | collective-permute-start | bytes 1179656 | tf_op jit(solution)/shard_map/ppermute | solution.py:200
  35.1 0.6 near_sums.1
  35.8 1.1 collective-permute-done.blocks
  36.8 1.7 %far_sums.1 = bf16[192,1536]{1,0:T(8,128)(2,1)S(1)} custom-call(f32[192,1536]{1,0:T(8,128)S(1)} %get-tuple-element.21.near, bf16[16,24,512]{2,1,0:T(8,128)(2,1)S(1)} %collective-permute-done.blocks, bf16[512,512]{1,0:T(8,128)(2,1)S(1)} %collective-permute-done.1.gate_weight, bf16[512,512]{1,0:T(8,128)(2,1)} %collective-permute-done.2.up_weight, ...), custom_call_target="tpu_custom_call" | custom-call | flops 301989888 | bytes 1769472 | tf_op jit(solution)/shard_map/far_sums/pallas_call | solution.py:134
  38.6 29.3 %all_to_all.26 = bf16[8,24,1536]{2,1,0:T(8,128)(2,1)S(1)} all-to-all(bf16[8,24,1536]{2,1,0:T(8,128)(2,1)S(1)} %bitcast.15), channel_id=1, replica_groups=mesh['y'=8,'x'=4,'z'=8,'core'=2] {'z'}, dimensions={0} | all-to-all | bytes 1179648 | tf_op jit(solution)/shard_map/all_to_all | solution.py:205
  68.1 20.8 %all_to_all.27 = bf16[8,24,1536]{2,1,0:T(8,128)(2,1)S(1)} all-to-all(bf16[8,24,1536]{2,1,0:T(8,128)(2,1)S(1)} %broadcast_in_dim.5), channel_id=1, replica_groups=mesh['y'=8,'x'=4,'z'=8,'core'=2] {'z'}, dimensions={0} | all-to-all | bytes 1179648 | tf_op jit(solution)/shard_map/all_to_all | solution.py:30
  88.9 1.9 %collective-permute-start.4 = (bf16[192,1536]{1,0:T(8,128)(2,1)S(1)}, bf16[192,1536]{1,0:T(8,128)(2,1)S(1)}, u32[]{:S(2)}, u32[]{:S(2)}) collective-permute-start(bf16[192,1536]{1,0:T(8,128)(2,1)S(1)} %bitcast.10), channel_id=1, source_target_pairs={{0,1},{1,0},{2,3},{3,2},{4,5},{5,4},{6,7},{7,6},{8,9},{9,8},{10,11... | collective-permute-start | bytes 1769480 | tf_op jit(solution)/shard_map/ppermute | solution.py:214
  90.8 1.4 %output_blocks.2.rest_0_ = bf16[32,24,512]{2,1,0:T(8,128)(2,1)} custom-call(s32[1]{0:T(128)} %bitcast.which, bf16[192,1536]{1,0:T(8,128)(2,1)S(1)} %bitcast.11, bf16[512,512]{1,0:T(8,128)(2,1)S(1)} %copy-done, bf16[512,512]{1,0:T(8,128)(2,1)S(1)} %copy-done.1, bf16[512,512]{1,0:T(8,128)(2,1)S(1)} %copy-done.2), custom_call_target="tpu_custom_call" | custom-call | flops 301989888 | bytes 393216 | tf_op jit(solution)/shard_map/output_blocks/pallas_call | solution.py:167
  92.1 0.6 collective-permute-done.4.part
  92.7 1.3 %output_blocks.3 = bf16[32,24,512]{2,1,0:T(8,128)(2,1)} custom-call(s32[1]{0:T(128)S(6)} %sub.6.which, bf16[192,1536]{1,0:T(8,128)(2,1)S(1)} %collective-permute-done.4.part, bf16[512,512]{1,0:T(8,128)(2,1)S(1)} %copy-done, bf16[512,512]{1,0:T(8,128)(2,1)S(1)} %copy-done.1, bf16[512,512]{1,0:T(8,128)(2,1)S(1)} %copy-done.2, ...), custom_call_target="tpu_custom_call", output_to_operand_aliasing={{}: (5, {})} | custom-call | flops 301989888 | bytes 393216 | tf_op jit(solution)/shard_map/output_blocks/pallas_call | solution.py:167
  94.1 5.8 %all-to-all-start.4 = ((bf16[32,24,512]{2,1,0:T(8,128)(2,1)}), bf16[32,24,512]{2,1,0:T(8,128)(2,1)S(1)}, u32[]{:S(2)}, u32[]{:S(2)}) async-start(bf16[32,24,512]{2,1,0:T(8,128)(2,1)} %output_blocks.3), calls=%async_computation.4 | async-start | bytes 1572864 | tf_op jit(solution)/shard_map/all_to_all | solution.py:217
  100.0 1.4 %fusion = f32[512,512]{1,0:T(8,128)} fusion(bf16[384,512]{1,0:T(8,128)(2,1)S(1)} %get-tuple-element.27, bf16[192,512]{1,0:T(8,128)(2,1)S(1)} %get-tuple-element.34, bf16[192,512]{1,0:T(8,128)(2,1)S(1)} %get-tuple-element.31), kind=kOutput, calls=%fused_computation | convolution fusion | flops 202113024 | bytes 1835008 | tf_op jit(solution)/shard_map/dot_general | solution.py:26
  101.4 1.4 %fusion.4 = f32[512,512]{1,0:T(8,128)} fusion(bf16[384,512]{1,0:T(8,128)(2,1)S(1)} %get-tuple-element.27, bf16[192,512]{1,0:T(8,128)(2,1)S(1)} %get-tuple-element.33, bf16[192,512]{1,0:T(8,128)(2,1)S(1)} %get-tuple-element.30), kind=kOutput, calls=%fused_computation.4 | convolution fusion | flops 202113024 | bytes 1835008 | tf_op jit(solution)/shard_map/dot_general | solution.py:26
  102.8 1.4 %fusion.8 = f32[512,512]{1,0:T(8,128)} fusion(bf16[384,512]{1,0:T(8,128)(2,1)S(1)} %copy-done.4, bf16[192,512]{1,0:T(8,128)(2,1)S(1)} %get-tuple-element.32, bf16[192,512]{1,0:T(8,128)(2,1)S(1)} %get-tuple-element.29), kind=kOutput, calls=%fused_computation.8 | convolution fusion | flops 202113024 | bytes 1835008 | tf_op jit(solution)/shard_map/dot_general | solution.py:26
  104.3 18.9 %all-to-all-done.4.blocks = bf16[32,24,512]{2,1,0:T(8,128)(2,1)S(1)} async-done(((bf16[32,24,512]{2,1,0:T(8,128)(2,1)}), bf16[32,24,512]{2,1,0:T(8,128)(2,1)S(1)}, u32[]{:S(2)}, u32[]{:S(2)}) %all-to-all-start.4) | async-done | bytes 786464 | tf_op jit(solution)/shard_map/all_to_all | solution.py:217
  123.2 0.7 totals.1
  (21 shorter events, 0.3 us)
Async XLA Ops:
  18.0 5.1 %copy-start = (bf16[512,512]{1,0:T(8,128)(2,1)S(1)}, bf16[512,512]{1,0:T(8,128)(2,1)}, u32[]{:S(2)}) copy-start(bf16[512,512]{1,0:T(8,128)(2,1)} %gate_weight.5) | copy-start | bytes 1572868
  18.0 7.0 %copy-start.1 = (bf16[512,512]{1,0:T(8,128)(2,1)S(1)}, bf16[512,512]{1,0:T(8,128)(2,1)}, u32[]{:S(2)}) copy-start(bf16[512,512]{1,0:T(8,128)(2,1)} %up_weight.5) | copy-start | bytes 1572868
  18.0 9.4 %copy-start.2 = (bf16[512,512]{1,0:T(8,128)(2,1)S(1)}, bf16[512,512]{1,0:T(8,128)(2,1)}, u32[]{:S(2)}) copy-start(bf16[512,512]{1,0:T(8,128)(2,1)} %down_weight.5) | copy-start | bytes 1572868
  18.9 14.3 %all-to-all-start.1 = ((bf16[4,8,24,512]{3,2,1,0:T(8,128)(2,1)}), bf16[4,8,24,512]{3,2,1,0:T(8,128)(2,1)S(1)}, u32[]{:S(2)}, u32[]{:S(2)}) async-start(bf16[4,8,24,512]{3,2,1,0:T(8,128)(2,1)} %broadcast_in_dim.4), calls=%async_computation.1 | async-start | bytes 1572864 | tf_op jit(solution)/shard_map/all_to_all | solution.py:30
  23.0 12.7 %collective-permute-start.1 = (bf16[512,512]{1,0:T(8,128)(2,1)S(1)}, bf16[512,512]{1,0:T(8,128)(2,1)S(1)}, u32[]{:S(2)}, u32[]{:S(2)}) collective-permute-start(bf16[512,512]{1,0:T(8,128)(2,1)S(1)} %copy-done), channel_id=1, source_target_pairs={{0,1},{1,0},{2,3},{3,2},{4,5},{5,4},{6,7},{7,6},{8,9},{9,8},{10,11... | collective-permute-start | bytes 1572872 | tf_op jit(solution)/shard_map/ppermute | solution.py:197
  24.9 10.8 %collective-permute-start.2 = (bf16[512,512]{1,0:T(8,128)(2,1)S(1)}, bf16[512,512]{1,0:T(8,128)(2,1)}, u32[]{:S(2)}, u32[]{:S(2)}) collective-permute-start(bf16[512,512]{1,0:T(8,128)(2,1)S(1)} %copy-done.1), channel_id=1, source_target_pairs={{0,1},{1,0},{2,3},{3,2},{4,5},{5,4},{6,7},{7,6},{8,9},{9,8},{10,11... | collective-permute-start | bytes 1572872 | tf_op jit(solution)/shard_map/ppermute | solution.py:197
  27.4 8.4 %collective-permute-start.3 = (bf16[512,512]{1,0:T(8,128)(2,1)S(1)}, bf16[512,512]{1,0:T(8,128)(2,1)}, u32[]{:S(2)}, u32[]{:S(2)}) collective-permute-start(bf16[512,512]{1,0:T(8,128)(2,1)S(1)} %copy-done.2), channel_id=1, source_target_pairs={{0,1},{1,0},{2,3},{3,2},{4,5},{5,4},{6,7},{7,6},{8,9},{9,8},{10,11... | collective-permute-start | bytes 1572872 | tf_op jit(solution)/shard_map/ppermute | solution.py:197
  33.2 3.6 %collective-permute-start = (bf16[16,24,512]{2,1,0:T(8,128)(2,1)S(1)}, bf16[16,24,512]{2,1,0:T(8,128)(2,1)S(1)}, u32[]{:S(2)}, u32[]{:S(2)}) collective-permute-start(bf16[16,24,512]{2,1,0:T(8,128)(2,1)S(1)} %constant_dynamic-slice_fusion), channel_id=1, source_target_pairs={{0,1},{1,0},{2,3},{3,2},{4,5},{5,4},{6,7},{7,6},{8,9},{9,8},{10,11... | collective-permute-start | bytes 1179656 | tf_op jit(solution)/shard_map/ppermute | solution.py:200
  35.7 2.9 %copy-start.3 = (bf16[384,512]{1,0:T(8,128)(2,1)}, bf16[384,512]{1,0:T(8,128)(2,1)S(1)}, u32[]{:S(2)}) copy-start(bf16[384,512]{1,0:T(8,128)(2,1)S(1)} %get-tuple-element.28) | copy-start | bytes 1179652
  88.9 3.9 %collective-permute-start.4 = (bf16[192,1536]{1,0:T(8,128)(2,1)S(1)}, bf16[192,1536]{1,0:T(8,128)(2,1)S(1)}, u32[]{:S(2)}, u32[]{:S(2)}) collective-permute-start(bf16[192,1536]{1,0:T(8,128)(2,1)S(1)} %bitcast.10), channel_id=1, source_target_pairs={{0,1},{1,0},{2,3},{3,2},{4,5},{5,4},{6,7},{7,6},{8,9},{9,8},{10,11... | collective-permute-start | bytes 1769480 | tf_op jit(solution)/shard_map/ppermute | solution.py:214
  94.1 29.1 %all-to-all-start.4 = ((bf16[32,24,512]{2,1,0:T(8,128)(2,1)}), bf16[32,24,512]{2,1,0:T(8,128)(2,1)S(1)}, u32[]{:S(2)}, u32[]{:S(2)}) async-start(bf16[32,24,512]{2,1,0:T(8,128)(2,1)} %output_blocks.3), calls=%async_computation.4 | async-start | bytes 1572864 | tf_op jit(solution)/shard_map/all_to_all | solution.py:217
  101.4 1.4 %copy-start.4 = (bf16[384,512]{1,0:T(8,128)(2,1)S(1)}, bf16[384,512]{1,0:T(8,128)(2,1)}, u32[]{:S(2)}) copy-start(bf16[384,512]{1,0:T(8,128)(2,1)} %copy-done.3) | copy-start | bytes 1179652

commit v4 on v3

--- a/solution.py
+++ b/solution.py
@@ -62,6 +62,26 @@
         compiler_params=PARAMS,
         name="pack",
     )(both)
+
+
+def fan_kernel(block, out, sems):
+    copies = [pltpu.make_async_copy(block, out.at[i], sems.at[i]) for i in range(out.shape[0])]
+    for copy in copies:
+        copy.start()
+    for copy in copies:
+        copy.wait()
+
+
+def fan(block, copies):
+    return pl.pallas_call(
+        fan_kernel,
+        out_shape=jax.ShapeDtypeStruct((copies,) + block.shape, BF16),
+        in_specs=[VM],
+        out_specs=pl.BlockSpec(memory_space=pl.ANY),
+        scratch_shapes=[pltpu.SemaphoreType.DMA((copies,))],
+        compiler_params=PARAMS,
+        name="fan",
+    )(block)
 
 
 def total_kernel(blocks, layer_out, input_grad):
@@ -121,11 +141,14 @@
     )(which, blocks, *weights)
 
 
-def far_kernel(near, blocks, gate_weight, up_weight, down_weight, out):
+def far_kernel(near, blocks, gate_weight, up_weight, down_in, out, down_weight, sem):
+    fetch = pltpu.make_async_copy(down_in, down_weight, sem)
+    fetch.start()
     h = gate_weight.shape[1]
     x, g = unpack(blocks, pl.ds(0, blocks.shape[0]))
     out[:, :h] = (near[:, :h] + mm(x, gate_weight[...])).astype(BF16)
     out[:, h : 2 * h] = (near[:, h : 2 * h] + mm(x, up_weight[...])).astype(BF16)
+    fetch.wait()
     out[:, 2 * h :] = (near[:, 2 * h :] + mm_t(g, down_weight[...])).astype(BF16)
 
 
@@ -134,8 +157,9 @@
     return pl.pallas_call(
         far_kernel,
         out_shape=jax.ShapeDtypeStruct(near.shape, BF16),
-        in_specs=[VM, VM, VM, VM, VM],
+        in_specs=[VM, VM, VM, VM, pl.BlockSpec(memory_space=pl.ANY)],
         out_specs=VM,
+        scratch_shapes=[pltpu.VMEM(weights[2].shape, BF16), pltpu.SemaphoreType.DMA],
         compiler_params=PARAMS,
         cost_estimate=pl.CostEstimate(flops=2 * n * width * blocks.shape[2], bytes_accessed=6 * n * width, transcendentals=0),
         name="far_sums",
@@ -195,7 +219,8 @@
     column = lax.all_to_all(both, "y", 0, 0)
     column, *moving = lax.optimization_barrier((column, *weights))
     far_weights = [lax.ppermute(w, "core", swap) for w in moving]
-    both = spread(column, "x", nx).reshape(rows, 24, d)
+    both = lax.all_to_all(fan(column, nx), "x", 0, 0).reshape(rows, 24, d)
+    both, far_weights = lax.optimization_barrier((both, far_weights))
     theirs = lax.dynamic_slice_in_dim(both, away[0] * (rows // nc), rows // nc, axis=0)
     far = lax.ppermute(theirs, "core", swap)
     near, x_cat, g_cat = near_sums(core, both, weights)

time: 124 us -> 124 us (level)
    all_to_all x1, waiting for transfers between devices: 3.88 us -> 1.87 us  [local(): both = lax.all_to_all(fan(column, nx), 'x', 0, 0).reshape(rows, 24, d)]
    ppermute x3, waiting for transfers between devices: 0.01 us -> 1.98 us  [local(): far_weights = [lax.ppermute(w, 'core', swap) for w in moving]]
  transfers between devices with their start and end apart: 7 -> 7, of which waited for: 4 -> 5; matrix products, arithmetic and copies ran while one was open for 4% -> 4% of each run, Pallas kernels for 2% -> 2%
where the time goes in v4:
time: 124 us
  blocking collectives  66.6 us (54%)
  waiting for transfers between devices  24.4 us (20%)
  starting transfers between devices  19.9 us (16%)
  Pallas kernels  6.38 us (5%)
  matrix products  4.29 us (3%)
    all_to_all x1, blocking collectives, local(): summed = add_up(lax.all_to_all(chip, 'z', 0, 0))  29.3 us
    all_to_all x1, blocking collectives, spread(): lax.all_to_all(jnp.broadcast_to(block[None], (size,) + block.shape), axis...  20.8 us
    all_to_all x1, waiting for transfers between devices, local(): layer_out, input_grad = totals(lax.all_to_all(blocks, ('x', 'y'), 0, 0))  18.9 us
    all_to_all x1, blocking collectives, local(): column = lax.all_to_all(both, 'y', 0, 0)  16.5 us
    ppermute x3, starting transfers between devices, local(): far_weights = [lax.ppermute(w, 'core', swap) for w in moving]  6.24 us
    all_to_all x1, starting transfers between devices, local(): layer_out, input_grad = totals(lax.all_to_all(blocks, ('x', 'y'), 0, 0))  5.74 us
    dot_general x3, matrix products, t_mm(): lax.dot_general(left, right, (((0,), (0,)), ((), ())), preferred_element_...  4.29 us
    all_to_all x1, starting transfers between devices, local(): both = lax.all_to_all(fan(column, nx), 'x', 0, 0).reshape(rows, 24, d)  4.12 us
  transfers between devices with their start and end apart: 7, of which 5 were waited for; matrix products, arithmetic and copies ran while one was open for 4% of the time, Pallas kernels for 2%

profile of v4, /device:TPU:8, one launch (start us, length us, event | category | flops | bytes accessed | tf_op | source)
XLA Modules:
  0.0 123.6 jit_solution(16756167764305398858)
XLA Ops:
  0.6 0.7 pad_maximum_fusion.1.both
  1.4 16.5 %all_to_all.25.block = bf16[8,24,512]{2,1,0:T(8,128)(2,1)S(1)} all-to-all(bf16[8,24,512]{2,1,0:T(8,128)(2,1)S(1)} %pack.1), channel_id=1, replica_groups=mesh['y'=8,'x'=4,'z'=8,'core'=2] {'y'}, dimensions={0} | all-to-all | bytes 393216 | tf_op jit(solution)/shard_map/all_to_all | solution.py:219
  18.0 0.9 fan.1
  18.9 4.1 %all-to-all-start.1 = ((bf16[4,8,24,512]{3,2,1,0:T(8,128)(2,1)}), bf16[4,8,24,512]{3,2,1,0:T(8,128)(2,1)S(1)}, u32[]{:S(2)}, u32[]{:S(2)}) async-start(bf16[4,8,24,512]{3,2,1,0:T(8,128)(2,1)} %fan.1), calls=%async_computation.1 | async-start | bytes 1572864 | tf_op jit(solution)/shard_map/all_to_all | solution.py:222
  23.0 1.9 %collective-permute-start = (bf16[512,512]{1,0:T(8,128)(2,1)S(1)}, bf16[512,512]{1,0:T(8,128)(2,1)S(1)}, u32[]{:S(2)}, u32[]{:S(2)}) collective-permute-start(bf16[512,512]{1,0:T(8,128)(2,1)S(1)} %copy-done), channel_id=1, source_target_pairs={{0,1},{1,0},{2,3},{3,2},{4,5},{5,4},{6,7},{7,6},{8,9},{9,8},{10,11... | collective-permute-start | bytes 1572872 | tf_op jit(solution)/shard_map/ppermute | solution.py:221
  24.9 2.4 %collective-permute-start.1 = (bf16[512,512]{1,0:T(8,128)(2,1)S(1)}, bf16[512,512]{1,0:T(8,128)(2,1)S(1)}, u32[]{:S(2)}, u32[]{:S(2)}) collective-permute-start(bf16[512,512]{1,0:T(8,128)(2,1)S(1)} %copy-done.1), channel_id=1, source_target_pairs={{0,1},{1,0},{2,3},{3,2},{4,5},{5,4},{6,7},{7,6},{8,9},{9,8},{10,11... | collective-permute-start | bytes 1572872 | tf_op jit(solution)/shard_map/ppermute | solution.py:221
  27.3 1.9 %collective-permute-start.2 = (bf16[512,512]{1,0:T(8,128)(2,1)S(1)}, bf16[512,512]{1,0:T(8,128)(2,1)}, u32[]{:S(2)}, u32[]{:S(2)}) collective-permute-start(bf16[512,512]{1,0:T(8,128)(2,1)S(1)} %copy-done.2), channel_id=1, source_target_pairs={{0,1},{1,0},{2,3},{3,2},{4,5},{5,4},{6,7},{7,6},{8,9},{9,8},{10,11... | collective-permute-start | bytes 1572872 | tf_op jit(solution)/shard_map/ppermute | solution.py:221
  29.3 2.0 %collective-permute-done.2.down_in = bf16[512,512]{1,0:T(8,128)(2,1)} collective-permute-done((bf16[512,512]{1,0:T(8,128)(2,1)S(1)}, bf16[512,512]{1,0:T(8,128)(2,1)}, u32[]{:S(2)}, u32[]{:S(2)}) %collective-permute-start.2) | collective-permute-done | bytes 524320 | tf_op jit(solution)/shard_map/ppermute | solution.py:221
  31.3 1.9 %all-to-all-done.1 = bf16[4,8,24,512]{3,2,1,0:T(8,128)(2,1)S(1)} async-done(((bf16[4,8,24,512]{3,2,1,0:T(8,128)(2,1)}), bf16[4,8,24,512]{3,2,1,0:T(8,128)(2,1)S(1)}, u32[]{:S(2)}, u32[]{:S(2)}) %all-to-all-start.1) | async-done | bytes 786464 | tf_op jit(solution)/shard_map/all_to_all | solution.py:222
  33.2 1.9 %collective-permute-start.3 = (bf16[16,24,512]{2,1,0:T(8,128)(2,1)S(1)}, bf16[16,24,512]{2,1,0:T(8,128)(2,1)S(1)}, u32[]{:S(2)}, u32[]{:S(2)}) collective-permute-start(bf16[16,24,512]{2,1,0:T(8,128)(2,1)S(1)} %constant_dynamic-slice_fusion), channel_id=1, source_target_pairs={{0,1},{1,0},{2,3},{3,2},{4,5},{5,4},{6,7},{7,6},{8,9},{9,8},{10,11... | collective-permute-start | bytes 1179656 | tf_op jit(solution)/shard_map/ppermute | solution.py:225
  35.7 1.1 collective-permute-done.3.blocks
  36.8 1.5 %far_sums.1 = bf16[192,1536]{1,0:T(8,128)(2,1)S(1)} custom-call(f32[192,1536]{1,0:T(8,128)S(1)} %get-tuple-element.29.near, bf16[16,24,512]{2,1,0:T(8,128)(2,1)S(1)} %collective-permute-done.3.blocks, bf16[512,512]{1,0:T(8,128)(2,1)S(1)} %collective-permute-done.gate_weight, bf16[512,512]{1,0:T(8,128)(2,1)S(1)} %copy-done.4, ...), custom_call_target="tpu_custom_call" | custom-call | flops 301989888 | bytes 1769472 | tf_op jit(solution)/shard_map/far_sums/pallas_call | solution.py:157
  38.3 29.3 %all_to_all.26 = bf16[8,24,1536]{2,1,0:T(8,128)(2,1)S(1)} all-to-all(bf16[8,24,1536]{2,1,0:T(8,128)(2,1)S(1)} %bitcast.15), channel_id=1, replica_groups=mesh['y'=8,'x'=4,'z'=8,'core'=2] {'z'}, dimensions={0} | all-to-all | bytes 1179648 | tf_op jit(solution)/shard_map/all_to_all | solution.py:230
  67.8 20.8 %all_to_all.27 = bf16[8,24,1536]{2,1,0:T(8,128)(2,1)S(1)} all-to-all(bf16[8,24,1536]{2,1,0:T(8,128)(2,1)S(1)} %broadcast_in_dim.2), channel_id=1, replica_groups=mesh['y'=8,'x'=4,'z'=8,'core'=2] {'z'}, dimensions={0} | all-to-all | bytes 1179648 | tf_op jit(solution)/shard_map/all_to_all | solution.py:30
  88.6 1.9 %collective-permute-start.4 = (bf16[192,1536]{1,0:T(8,128)(2,1)S(1)}, bf16[192,1536]{1,0:T(8,128)(2,1)S(1)}, u32[]{:S(2)}, u32[]{:S(2)}) collective-permute-start(bf16[192,1536]{1,0:T(8,128)(2,1)S(1)} %bitcast.10), channel_id=1, source_target_pairs={{0,1},{1,0},{2,3},{3,2},{4,5},{5,4},{6,7},{7,6},{8,9},{9,8},{10,11... | collective-permute-start | bytes 1769480 | tf_op jit(solution)/shard_map/ppermute | solution.py:239
  90.5 1.4 %output_blocks.2.rest_0_ = bf16[32,24,512]{2,1,0:T(8,128)(2,1)} custom-call(s32[1]{0:T(128)} %bitcast.which, bf16[192,1536]{1,0:T(8,128)(2,1)S(1)} %bitcast.11, bf16[512,512]{1,0:T(8,128)(2,1)S(1)} %copy-done, bf16[512,512]{1,0:T(8,128)(2,1)S(1)} %copy-done.1, bf16[512,512]{1,0:T(8,128)(2,1)S(1)} %copy-done.2), custom_call_target="tpu_custom_call" | custom-call | flops 301989888 | bytes 393216 | tf_op jit(solution)/shard_map/output_blocks/pallas_call | solution.py:191
  91.9 0.6 collective-permute-done.4.part
  92.5 1.3 %output_blocks.3 = bf16[32,24,512]{2,1,0:T(8,128)(2,1)} custom-call(s32[1]{0:T(128)S(6)} %sub.6.which, bf16[192,1536]{1,0:T(8,128)(2,1)S(1)} %collective-permute-done.4.part, bf16[512,512]{1,0:T(8,128)(2,1)S(1)} %copy-done, bf16[512,512]{1,0:T(8,128)(2,1)S(1)} %copy-done.1, bf16[512,512]{1,0:T(8,128)(2,1)S(1)} %copy-done.2, ...), custom_call_target="tpu_custom_call", output_to_operand_aliasing={{}: (5, {})} | custom-call | flops 301989888 | bytes 393216 | tf_op jit(solution)/shard_map/output_blocks/pallas_call | solution.py:191
  93.8 5.7 %all-to-all-start.4 = ((bf16[32,24,512]{2,1,0:T(8,128)(2,1)}), bf16[32,24,512]{2,1,0:T(8,128)(2,1)S(1)}, u32[]{:S(2)}, u32[]{:S(2)}) async-start(bf16[32,24,512]{2,1,0:T(8,128)(2,1)} %output_blocks.3), calls=%async_computation.4 | async-start | bytes 1572864 | tf_op jit(solution)/shard_map/all_to_all | solution.py:242
  99.7 1.4 %fusion.4 = f32[512,512]{1,0:T(8,128)} fusion(bf16[384,512]{1,0:T(8,128)(2,1)S(1)} %get-tuple-element.35, bf16[192,512]{1,0:T(8,128)(2,1)S(1)} %get-tuple-element.41, bf16[192,512]{1,0:T(8,128)(2,1)S(1)} %get-tuple-element.38), kind=kOutput, calls=%fused_computation.4 | convolution fusion | flops 202113024 | bytes 1835008 | tf_op jit(solution)/shard_map/dot_general | solution.py:26
  101.1 1.4 %fusion = f32[512,512]{1,0:T(8,128)} fusion(bf16[384,512]{1,0:T(8,128)(2,1)S(1)} %get-tuple-element.35, bf16[192,512]{1,0:T(8,128)(2,1)S(1)} %get-tuple-element.42, bf16[192,512]{1,0:T(8,128)(2,1)S(1)} %get-tuple-element.39), kind=kOutput, calls=%fused_computation | convolution fusion | flops 202113024 | bytes 1835008 | tf_op jit(solution)/shard_map/dot_general | solution.py:26
  102.5 1.4 %fusion.8 = f32[512,512]{1,0:T(8,128)} fusion(bf16[384,512]{1,0:T(8,128)(2,1)S(1)} %copy-done.6, bf16[192,512]{1,0:T(8,128)(2,1)S(1)} %get-tuple-element.40, bf16[192,512]{1,0:T(8,128)(2,1)S(1)} %get-tuple-element.37), kind=kOutput, calls=%fused_computation.8 | convolution fusion | flops 202113024 | bytes 1835008 | tf_op jit(solution)/shard_map/dot_general | solution.py:26
  104.0 18.9 %all-to-all-done.4.blocks = bf16[32,24,512]{2,1,0:T(8,128)(2,1)S(1)} async-done(((bf16[32,24,512]{2,1,0:T(8,128)(2,1)}), bf16[32,24,512]{2,1,0:T(8,128)(2,1)S(1)}, u32[]{:S(2)}, u32[]{:S(2)}) %all-to-all-start.4) | async-done | bytes 786464 | tf_op jit(solution)/shard_map/all_to_all | solution.py:242
  122.9 0.7 totals.1
  (25 shorter events, 0.9 us)
Async XLA Ops:
  18.0 5.0 %copy-start = (bf16[512,512]{1,0:T(8,128)(2,1)S(1)}, bf16[512,512]{1,0:T(8,128)(2,1)}, u32[]{:S(2)}) copy-start(bf16[512,512]{1,0:T(8,128)(2,1)} %gate_weight.5) | copy-start | bytes 1572868
  18.0 7.0 %copy-start.1 = (bf16[512,512]{1,0:T(8,128)(2,1)S(1)}, bf16[512,512]{1,0:T(8,128)(2,1)}, u32[]{:S(2)}) copy-start(bf16[512,512]{1,0:T(8,128)(2,1)} %up_weight.5) | copy-start | bytes 1572868
  18.0 9.4 %copy-start.2 = (bf16[512,512]{1,0:T(8,128)(2,1)S(1)}, bf16[512,512]{1,0:T(8,128)(2,1)}, u32[]{:S(2)}) copy-start(bf16[512,512]{1,0:T(8,128)(2,1)} %down_weight.5) | copy-start | bytes 1572868
  18.9 14.3 %all-to-all-start.1 = ((bf16[4,8,24,512]{3,2,1,0:T(8,128)(2,1)}), bf16[4,8,24,512]{3,2,1,0:T(8,128)(2,1)S(1)}, u32[]{:S(2)}, u32[]{:S(2)}) async-start(bf16[4,8,24,512]{3,2,1,0:T(8,128)(2,1)} %fan.1), calls=%async_computation.1 | async-start | bytes 1572864 | tf_op jit(solution)/shard_map/all_to_all | solution.py:222
  23.0 6.3 %collective-permute-start = (bf16[512,512]{1,0:T(8,128)(2,1)S(1)}, bf16[512,512]{1,0:T(8,128)(2,1)S(1)}, u32[]{:S(2)}, u32[]{:S(2)}) collective-permute-start(bf16[512,512]{1,0:T(8,128)(2,1)S(1)} %copy-done), channel_id=1, source_target_pairs={{0,1},{1,0},{2,3},{3,2},{4,5},{5,4},{6,7},{7,6},{8,9},{9,8},{10,11... | collective-permute-start | bytes 1572872 | tf_op jit(solution)/shard_map/ppermute | solution.py:221
  24.9 4.4 %collective-permute-start.1 = (bf16[512,512]{1,0:T(8,128)(2,1)S(1)}, bf16[512,512]{1,0:T(8,128)(2,1)S(1)}, u32[]{:S(2)}, u32[]{:S(2)}) collective-permute-start(bf16[512,512]{1,0:T(8,128)(2,1)S(1)} %copy-done.1), channel_id=1, source_target_pairs={{0,1},{1,0},{2,3},{3,2},{4,5},{5,4},{6,7},{7,6},{8,9},{9,8},{10,11... | collective-permute-start | bytes 1572872 | tf_op jit(solution)/shard_map/ppermute | solution.py:221
  27.3 3.9 %collective-permute-start.2 = (bf16[512,512]{1,0:T(8,128)(2,1)S(1)}, bf16[512,512]{1,0:T(8,128)(2,1)}, u32[]{:S(2)}, u32[]{:S(2)}) collective-permute-start(bf16[512,512]{1,0:T(8,128)(2,1)S(1)} %copy-done.2), channel_id=1, source_target_pairs={{0,1},{1,0},{2,3},{3,2},{4,5},{5,4},{6,7},{7,6},{8,9},{9,8},{10,11... | collective-permute-start | bytes 1572872 | tf_op jit(solution)/shard_map/ppermute | solution.py:221
  29.3 3.9 %copy-start.3 = (bf16[512,512]{1,0:T(8,128)(2,1)}, bf16[512,512]{1,0:T(8,128)(2,1)S(1)}, u32[]{:S(2)}) copy-start(bf16[512,512]{1,0:T(8,128)(2,1)S(1)} %collective-permute-done.1.up_weight) | copy-start | bytes 1572868
  33.2 3.6 %collective-permute-start.3 = (bf16[16,24,512]{2,1,0:T(8,128)(2,1)S(1)}, bf16[16,24,512]{2,1,0:T(8,128)(2,1)S(1)}, u32[]{:S(2)}, u32[]{:S(2)}) collective-permute-start(bf16[16,24,512]{2,1,0:T(8,128)(2,1)S(1)} %constant_dynamic-slice_fusion), channel_id=1, source_target_pairs={{0,1},{1,0},{2,3},{3,2},{4,5},{5,4},{6,7},{7,6},{8,9},{9,8},{10,11... | collective-permute-start | bytes 1179656 | tf_op jit(solution)/shard_map/ppermute | solution.py:225
  35.1 1.7 %copy-start.4 = (bf16[512,512]{1,0:T(8,128)(2,1)S(1)}, bf16[512,512]{1,0:T(8,128)(2,1)}, u32[]{:S(2)}) copy-start(bf16[512,512]{1,0:T(8,128)(2,1)} %copy-done.3) | copy-start | bytes 1572868
  35.7 2.6 %copy-start.5 = (bf16[384,512]{1,0:T(8,128)(2,1)}, bf16[384,512]{1,0:T(8,128)(2,1)S(1)}, u32[]{:S(2)}) copy-start(bf16[384,512]{1,0:T(8,128)(2,1)S(1)} %get-tuple-element.36) | copy-start | bytes 1179652
  88.6 3.9 %collective-permute-start.4 = (bf16[192,1536]{1,0:T(8,128)(2,1)S(1)}, bf16[192,1536]{1,0:T(8,128)(2,1)S(1)}, u32[]{:S(2)}, u32[]{:S(2)}) collective-permute-start(bf16[192,1536]{1,0:T(8,128)(2,1)S(1)} %bitcast.10), channel_id=1, source_target_pairs={{0,1},{1,0},{2,3},{3,2},{4,5},{5,4},{6,7},{7,6},{8,9},{9,8},{10,11... | collective-permute-start | bytes 1769480 | tf_op jit(solution)/shard_map/ppermute | solution.py:239
  93.8 29.0 %all-to-all-start.4 = ((bf16[32,24,512]{2,1,0:T(8,128)(2,1)}), bf16[32,24,512]{2,1,0:T(8,128)(2,1)S(1)}, u32[]{:S(2)}, u32[]{:S(2)}) async-start(bf16[32,24,512]{2,1,0:T(8,128)(2,1)} %output_blocks.3), calls=%async_computation.4 | async-start | bytes 1572864 | tf_op jit(solution)/shard_map/all_to_all | solution.py:242
  101.1 1.4 %copy-start.6 = (bf16[384,512]{1,0:T(8,128)(2,1)S(1)}, bf16[384,512]{1,0:T(8,128)(2,1)}, u32[]{:S(2)}) copy-start(bf16[384,512]{1,0:T(8,128)(2,1)} %copy-done.5) | copy-start | bytes 1179652

commit v5 on v2

--- a/solution.py
+++ b/solution.py
@@ -120,32 +120,38 @@
     out = rest[-1]
     h = gate_weight.shape[1]
     d = gate_weight.shape[0]
-    m = out.shape[0]
+    ny, nx = out.shape[:2]
+    m = ny * nx
     f = mm(part[:, :h], down_weight[...])
     b = mm_t(part[:, h : 2 * h], gate_weight[...]) + mm_t(part[:, 2 * h :], up_weight[...])
-    out[:, 0:8, :] = f[: m * 8].reshape(m, 8, d).astype(BF16)
-    out[:, 8:16, :] = b[: m * 8].reshape(m, 8, d).astype(BF16)
+    f_head = f[: m * 8].reshape(m, 8, d).astype(BF16)
+    b_head = b[: m * 8].reshape(m, 8, d).astype(BF16)
     f = f[m * 8 :].reshape(m // 2, 8, d)
     b = b[m * 8 :].reshape(m // 2, 8, d)
     low = low_rows(f.shape)
     even = jnp.where(low, f, pltpu.roll(b, 4, 1))
     odd = jnp.where(low, pltpu.roll(f, 4, 1), b)
-    out[:, 16:24, :] = jnp.concatenate([even, odd], axis=1).reshape(m, 8, d).astype(BF16)
-
-
-def output_blocks(which, part, weights, blocks=None):
+    tail = jnp.concatenate([even, odd], axis=1).reshape(m, 8, d).astype(BF16)
+    for x in range(nx):
+        rows = slice(x * ny, (x + 1) * ny)
+        out[:, x, 0:8, :] = f_head[rows]
+        out[:, x, 8:16, :] = b_head[rows]
+        out[:, x, 16:24, :] = tail[rows]
+
+
+def output_blocks(which, part, weights, ny, blocks=None):
     n, width = part.shape
     d = weights[0].shape[0]
-    m = n // 12
+    nx = n // 12 // ny
     more = [] if blocks is None else [blocks]
     return pl.pallas_call(
         output_kernel,
-        out_shape=jax.ShapeDtypeStruct((2 * m, 24, d), BF16),
+        out_shape=jax.ShapeDtypeStruct((ny, 2 * nx, 24, d), BF16),
         grid_spec=pltpu.PrefetchScalarGridSpec(
             num_scalar_prefetch=1,
             grid=(1,),
             in_specs=[VM, VM, VM, VM] + [pl.BlockSpec(memory_space=pl.ANY)] * len(more),
-            out_specs=pl.BlockSpec((m, 24, d), lambda i, which: (which[0], 0, 0)),
+            out_specs=pl.BlockSpec((ny, nx, 24, d), lambda i, which: (0, which[0], 0, 0)),
         ),
         input_output_aliases={5: 0} if more else {},
         compiler_params=PARAMS,
@@ -183,9 +189,9 @@
     mine = jnp.concatenate([hidden, gate_delta, up_delta], axis=1)
     own = spread(mine, "z", nz).reshape(half, 3 * h)
     other = lax.ppermute(own, "core", swap)
-    blocks = output_blocks(core, own, weights)
-    blocks = output_blocks(away, other, weights, blocks)
-    layer_out, input_grad = totals(lax.all_to_all(blocks, ("x", "y"), 0, 0))
+    blocks = output_blocks(core, own, weights, ny)
+    blocks = output_blocks(away, other, weights, ny, blocks).reshape(rows, 24, d)
+    layer_out, input_grad = totals(lax.all_to_all(blocks, ("y", "x"), 0, 0))
 
     hid, gd, ud = (jnp.concatenate([own[:, i * h : (i + 1) * h], other[:, i * h : (i + 1) * h]], axis=0) for i in range(3))
     x_cat = jnp.concatenate([x_own, x_other], axis=0)

time: 123 us -> 123 us (level)
  the two profiles are of different devices: /device:TPU:8 before, /device:TPU:2 now
where the time goes in v5:
time: 123 us
  blocking collectives  81.1 us (66%)
  waiting for transfers between devices  21.1 us (17%)
  starting transfers between devices  9.42 us (8%)
  Pallas kernels  4.61 us (4%)
  matrix products  4.31 us (4%)
    all_to_all x2, blocking collectives, spread(): lax.all_to_all(jnp.broadcast_to(block[None], (size,) + block.shape), axis...  34.4 us
    all_to_all x1, blocking collectives, local(): summed = add_up(lax.all_to_all(chip, 'z', 0, 0))  29.3 us
    all_to_all x1, waiting for transfers between devices, local(): layer_out, input_grad = totals(lax.all_to_all(blocks, ('y', 'x'), 0, 0))  18.3 us
    all_to_all x1, blocking collectives, local(): both = spread(lax.all_to_all(both, 'y', 0, 0), 'x', nx).reshape(rows, 24, d)  17.4 us
    all_to_all x1, starting transfers between devices, local(): layer_out, input_grad = totals(lax.all_to_all(blocks, ('y', 'x'), 0, 0))  5.59 us
    dot_general x3, matrix products, t_mm(): lax.dot_general(left, right, (((0,), (0,)), ((), ())), preferred_element_...  4.31 us
    pallas_call x2, Pallas kernels, output_blocks(): pl.pallas_call(output_kernel, out_shape=jax.ShapeDtypeStruct((ny, 2 * nx,...  2.79 us
  transfers between devices with their start and end apart: 3, of which 3 were waited for; matrix products, arithmetic and copies ran while one was open for 4% of the time, Pallas kernels for 2%

profile of v5, /device:TPU:2, one launch (start us, length us, event | category | flops | bytes accessed | tf_op | source)
XLA Modules:
  0.0 122.5 jit_solution(2717832022497055282)
XLA Ops:
  0.6 0.7 pad_maximum_fusion.1.both
  1.4 17.4 %all_to_all.25 = bf16[8,24,512]{2,1,0:T(8,128)(2,1)S(1)} all-to-all(bf16[8,24,512]{2,1,0:T(8,128)(2,1)S(1)} %pack.1), channel_id=1, replica_groups=mesh['y'=8,'x'=4,'z'=8,'core'=2] {'y'}, dimensions={0} | all-to-all | bytes 393216 | tf_op jit(solution)/shard_map/all_to_all | solution.py:174
  18.8 0.1 broadcast_in_dim.4
  18.9 13.6 %all_to_all.26 = bf16[4,8,24,512]{3,2,1,0:T(8,128)(2,1)S(1)} all-to-all(bf16[4,8,24,512]{3,2,1,0:T(8,128)(2,1)S(1)} %broadcast_in_dim.4), channel_id=1, replica_groups=mesh['y'=8,'x'=4,'z'=8,'core'=2] {'x'}, dimensions={0} | all-to-all | bytes 1572864 | tf_op jit(solution)/shard_map/all_to_all | solution.py:30
  32.5 0.0 copy-done
  32.5 0.0 copy-done.2
  32.5 0.5 partial_sums.3
  33.1 1.9 %collective-permute-start = (f32[192,1536]{1,0:T(8,128)S(1)}, f32[192,1536]{1,0:T(8,128)S(1)}, u32[]{:S(2)}, u32[]{:S(2)}) collective-permute-start(f32[192,1536]{1,0:T(8,128)S(1)} %get-tuple-element.20), channel_id=1, source_target_pairs={{0,1},{1,0},{2,3},{3,2},{4,5},{5,4},{6,7},{7,6},{8,9},{9,8},{10,11... | collective-permute-start | bytes 3538952 | tf_op jit(solution)/shard_map/ppermute | solution.py:177
  35.0 0.5 partial_sums.2
  35.5 2.3 %collective-permute-done = f32[192,1536]{1,0:T(8,128)S(1)} collective-permute-done((f32[192,1536]{1,0:T(8,128)S(1)}, f32[192,1536]{1,0:T(8,128)S(1)}, u32[]{:S(2)}, u32[]{:S(2)}) %collective-permute-start) | collective-permute-done | bytes 1179680 | tf_op jit(solution)/shard_map/ppermute | solution.py:177
  37.8 0.1 add_convert_fusion
  37.9 29.3 %all_to_all.27 = bf16[8,24,1536]{2,1,0:T(8,128)(2,1)S(1)} all-to-all(bf16[8,24,1536]{2,1,0:T(8,128)(2,1)S(1)} %bitcast.14), channel_id=1, replica_groups=mesh['y'=8,'x'=4,'z'=8,'core'=2] {'z'}, dimensions={0} | all-to-all | bytes 1179648 | tf_op jit(solution)/shard_map/all_to_all | solution.py:182
  67.2 0.1 add_bitcast_fusion
  67.4 20.8 %all_to_all.28 = bf16[8,24,1536]{2,1,0:T(8,128)(2,1)S(1)} all-to-all(bf16[8,24,1536]{2,1,0:T(8,128)(2,1)S(1)} %broadcast_in_dim.5), channel_id=1, replica_groups=mesh['y'=8,'x'=4,'z'=8,'core'=2] {'z'}, dimensions={0} | all-to-all | bytes 1179648 | tf_op jit(solution)/shard_map/all_to_all | solution.py:30
  88.2 1.9 %collective-permute-start.1 = (bf16[192,1536]{1,0:T(8,128)(2,1)S(1)}, bf16[192,1536]{1,0:T(8,128)(2,1)S(1)}, u32[]{:S(2)}, u32[]{:S(2)}) collective-permute-start(bf16[192,1536]{1,0:T(8,128)(2,1)S(1)} %bitcast.11), channel_id=1, source_target_pairs={{0,1},{1,0},{2,3},{3,2},{4,5},{5,4},{6,7},{7,6},{8,9},{9,8},{10,11... | collective-permute-start | bytes 1769480 | tf_op jit(solution)/shard_map/ppermute | solution.py:191
  90.1 1.4 %output_blocks.2.rest_0_ = bf16[8,4,24,512]{3,2,1,0:T(8,128)(2,1)} custom-call(s32[1]{0:T(128)} %bitcast.which, bf16[192,1536]{1,0:T(8,128)(2,1)S(1)} %bitcast.12, bf16[512,512]{1,0:T(8,128)(2,1)S(1)} %copy-done, bf16[512,512]{1,0:T(8,128)(2,1)S(1)} %copy-done.1, bf16[512,512]{1,0:T(8,128)(2,1)S(1)} %copy-done.2), custom_call_target="tpu_custom_call" | custom-call | flops 301989888 | bytes 393216 | tf_op jit(solution)/shard_map/output_blocks/pallas_call | solution.py:147
  91.5 0.6 collective-permute-done.1.part
  92.1 1.4 %output_blocks.3 = bf16[8,4,24,512]{3,2,1,0:T(8,128)(2,1)} custom-call(s32[1]{0:T(128)S(6)} %sub.6.which, bf16[192,1536]{1,0:T(8,128)(2,1)S(1)} %collective-permute-done.1.part, bf16[512,512]{1,0:T(8,128)(2,1)S(1)} %copy-done, bf16[512,512]{1,0:T(8,128)(2,1)S(1)} %copy-done.1, bf16[512,512]{1,0:T(8,128)(2,1)S(1)} %copy-done.2, ...), custom_call_target="tpu_custom_call", output_to_operand_aliasing={{}: (5, {})} | custom-call | flops 301989888 | bytes 393216 | tf_op jit(solution)/shard_map/output_blocks/pallas_call | solution.py:147
  93.5 5.6 %all-to-all-start.4 = ((bf16[32,24,512]{2,1,0:T(8,128)(2,1)}), bf16[32,24,512]{2,1,0:T(8,128)(2,1)S(1)}, u32[]{:S(2)}, u32[]{:S(2)}) async-start(bf16[32,24,512]{2,1,0:T(8,128)(2,1)} %bitcast.5), calls=%async_computation.4 | async-start | bytes 1572864 | tf_op jit(solution)/shard_map/all_to_all | solution.py:194
  99.2 1.4 %fusion.8 = f32[512,512]{1,0:T(8,128)} fusion(bf16[192,512]{1,0:T(8,128)(2,1)S(1)} %get-tuple-element.30, bf16[192,512]{1,0:T(8,128)(2,1)S(1)} %get-tuple-element.27, bf16[192,512]{1,0:T(8,128)(2,1)S(1)} %get-tuple-element.26, bf16[192,512]{1,0:T(8,128)(2,1)S(1)} %get-tuple-element.25), kind=kOutput, calls=%fused_computation.9 | convolution fusion | flops 202899456 | bytes 1835008 | tf_op jit(solution)/shard_map/dot_general | solution.py:26
  100.7 1.4 %fusion = f32[512,512]{1,0:T(8,128)} fusion(bf16[384,512]{1,0:T(8,128)(2,1)S(1)} %constant_dynamic-update-slice_fusion, bf16[192,512]{1,0:T(8,128)(2,1)S(1)} %get-tuple-element.32, bf16[192,512]{1,0:T(8,128)(2,1)S(1)} %get-tuple-element.29), kind=kOutput, calls=%fused_computation.1 | convolution fusion | flops 202113024 | bytes 1835008 | tf_op jit(solution)/shard_map/dot_general | solution.py:26
  102.1 1.4 %fusion.4 = f32[512,512]{1,0:T(8,128)} fusion(bf16[384,512]{1,0:T(8,128)(2,1)S(1)} %constant_dynamic-update-slice_fusion, bf16[192,512]{1,0:T(8,128)(2,1)S(1)} %get-tuple-element.31, bf16[192,512]{1,0:T(8,128)(2,1)S(1)} %get-tuple-element.28), kind=kOutput, calls=%fused_computation.5 | convolution fusion | flops 202113024 | bytes 1835008 | tf_op jit(solution)/shard_map/dot_general | solution.py:26
  103.5 18.3 %all-to-all-done.4.blocks = bf16[32,24,512]{2,1,0:T(8,128)(2,1)S(1)} async-done(((bf16[32,24,512]{2,1,0:T(8,128)(2,1)}), bf16[32,24,512]{2,1,0:T(8,128)(2,1)S(1)}, u32[]{:S(2)}, u32[]{:S(2)}) %all-to-all-start.4) | async-done | bytes 786464 | tf_op jit(solution)/shard_map/all_to_all | solution.py:194
  121.8 0.7 totals.1
  (12 shorter events, 0.2 us)
Async XLA Ops:
  18.8 13.7 %copy-start = (bf16[512,512]{1,0:T(8,128)(2,1)S(1)}, bf16[512,512]{1,0:T(8,128)(2,1)}, u32[]{:S(2)}) copy-start(bf16[512,512]{1,0:T(8,128)(2,1)} %gate_weight.7) | copy-start | bytes 1572868
  18.8 13.7 %copy-start.1 = (bf16[512,512]{1,0:T(8,128)(2,1)S(1)}, bf16[512,512]{1,0:T(8,128)(2,1)}, u32[]{:S(2)}) copy-start(bf16[512,512]{1,0:T(8,128)(2,1)} %up_weight.7) | copy-start | bytes 1572868
  18.8 13.7 %copy-start.2 = (bf16[512,512]{1,0:T(8,128)(2,1)S(1)}, bf16[512,512]{1,0:T(8,128)(2,1)}, u32[]{:S(2)}) copy-start(bf16[512,512]{1,0:T(8,128)(2,1)} %down_weight.7) | copy-start | bytes 1572868
  33.1 4.7 %collective-permute-start = (f32[192,1536]{1,0:T(8,128)S(1)}, f32[192,1536]{1,0:T(8,128)S(1)}, u32[]{:S(2)}, u32[]{:S(2)}) collective-permute-start(f32[192,1536]{1,0:T(8,128)S(1)} %get-tuple-element.20), channel_id=1, source_target_pairs={{0,1},{1,0},{2,3},{3,2},{4,5},{5,4},{6,7},{7,6},{8,9},{9,8},{10,11... | collective-permute-start | bytes 3538952 | tf_op jit(solution)/shard_map/ppermute | solution.py:177
  88.2 3.9 %collective-permute-start.1 = (bf16[192,1536]{1,0:T(8,128)(2,1)S(1)}, bf16[192,1536]{1,0:T(8,128)(2,1)S(1)}, u32[]{:S(2)}, u32[]{:S(2)}) collective-permute-start(bf16[192,1536]{1,0:T(8,128)(2,1)S(1)} %bitcast.11), channel_id=1, source_target_pairs={{0,1},{1,0},{2,3},{3,2},{4,5},{5,4},{6,7},{7,6},{8,9},{9,8},{10,11... | collective-permute-start | bytes 1769480 | tf_op jit(solution)/shard_map/ppermute | solution.py:191
  93.5 28.3 %all-to-all-start.4 = ((bf16[32,24,512]{2,1,0:T(8,128)(2,1)}), bf16[32,24,512]{2,1,0:T(8,128)(2,1)S(1)}, u32[]{:S(2)}, u32[]{:S(2)}) async-start(bf16[32,24,512]{2,1,0:T(8,128)(2,1)} %bitcast.5), calls=%async_computation.4 | async-start | bytes 1572864 | tf_op jit(solution)/shard_map/all_to_all | solution.py:194
